TPU v7x, 32 devices: a whole 2x2x4 slice. The times are simulated.
32 devices in a mesh: gx: 8 (over y, x, core), gy: 4 (over z).
Axes of the slice: x: 2, y: 2, z: 4, core: 2. Of those that a mesh axis runs over, the one named last changes fastest.
Arguments:
- e_field: float32 [3, 3, 2048, 2048], P(None, None, 'gx', 'gy'), may hold values from -6 to 6
- h_field: float32 [3, 3, 2048, 2048], P(None, None, 'gx', 'gy'), may hold values from -6 to 6
- material: int32 [3, 2048, 2048], P(None, 'gx', 'gy'), may hold values from 0 to 7
- eps_table: float32 [8], replicated, may hold values from 1 to 12
- src_pos: int32 [1024, 3], replicated, may hold values from 0 to 2047, as said below
- src_amp: float32 [1024], replicated, may hold values from -40 to 40
- freqs: float32 [2], replicated, may hold values from 0.3 to 2.8
Outputs:
- e_out: float32 [3, 3, 2048, 2048], P(None, None, 'gx', 'gy')
- h_out: float32 [3, 3, 2048, 2048], P(None, None, 'gx', 'gy')
- far_field: float32 [1024, 8, 2, 1024], P('gx', None, None, 'gy')
Inputs may be any that keep to these rules, and one draw needn't show every extreme that they name: `src_pos`: each row is a cell (layer, row, column) of the slab; several sources may share a cell.
All inputs are finite; a program needn't handle non-finite values.
Results may differ from a plain program's by a relative error of at most 0.0054.
Values may be sent and summed in bfloat16 or wider, within the bound.
A program may use at most 192 MiB of HBM per device.

v0:
```python
import math

import jax
import jax.numpy as jnp
from jax import lax
from jax.sharding import PartitionSpec as P

LZ = 3
FACE = 1
STEPS = 2
NF = 2
NA = 1024
NMAT = 8


courant = 0.5
source_rate = 0.7
zoom_factor = 4


def shifted(block, axis, distance):
    devices = range(lax.axis_size(axis))
    route = [(i - distance, i) for i in devices if i - distance in devices]
    return lax.ppermute(block, axis, route)


def chirp(freq_index, cell_index, period):
    remainder = jnp.remainder(freq_index * cell_index, period)
    phase_angle = remainder.astype(jnp.float32) * (2.0 * math.pi / period)
    return (jnp.cos(phase_angle), -jnp.sin(phase_angle))


def forward(field, dimension, boundary):
    inner = lax.slice_in_dim(field, 1, field.shape[dimension], axis=dimension)
    return jnp.concatenate([inner, jnp.expand_dims(boundary, dimension)], dimension)


def backward(field, dimension, boundary):
    inner = lax.slice_in_dim(field, 0, field.shape[dimension] - 1, axis=dimension)
    return jnp.concatenate([jnp.expand_dims(boundary, dimension), inner], dimension)


def curl_forward(electric, row_rim, col_rim):
    field_x, field_y, field_z = (electric[0], electric[1], electric[2])
    zero_layer = jnp.zeros(field_x.shape[1:], jnp.float32)
    curl_x = forward(field_z, 2, col_rim[1]) - field_z - (forward(field_y, 0, zero_layer) - field_y)
    curl_y = forward(field_x, 0, zero_layer) - field_x - (forward(field_z, 1, row_rim[1]) - field_z)
    curl_z = forward(field_y, 1, row_rim[0]) - field_y - (forward(field_x, 2, col_rim[0]) - field_x)
    return jnp.stack([curl_x, curl_y, curl_z])


def curl_backward(magnetic, row_rim, col_rim):
    field_x, field_y, field_z = (magnetic[0], magnetic[1], magnetic[2])
    zero_layer = jnp.zeros(field_x.shape[1:], jnp.float32)
    curl_x = (
        field_z - backward(field_z, 2, col_rim[1]) - (field_y - backward(field_y, 0, zero_layer))
    )
    curl_y = (
        field_x - backward(field_x, 0, zero_layer) - (field_z - backward(field_z, 1, row_rim[1]))
    )
    curl_z = (
        field_y - backward(field_y, 1, row_rim[0]) - (field_x - backward(field_x, 2, col_rim[0]))
    )
    return jnp.stack([curl_x, curl_y, curl_z])


def complex_pair(product_re_re, product_re_im, product_im_re, product_im_im):
    return (product_re_re - product_im_im, product_re_im + product_im_re)


def on_device(e_field, h_field, material, eps_table, src_pos, src_amp, freqs):
    row_count = e_field.shape[2]
    col_count = e_field.shape[3]
    grid_rows = row_count * lax.axis_size("gx")
    grid_cols = col_count * lax.axis_size("gy")
    row_start = lax.axis_index("gx") * row_count
    col_start = lax.axis_index("gy") * col_count
    permittivity = jnp.zeros(material.shape, jnp.float32)
    for material_id in range(NMAT):
        permittivity = permittivity + jnp.where(
            material == material_id, eps_table[material_id], 0.0
        )
    update_scale = courant / permittivity
    local_row = src_pos[:, 1] - row_start
    local_col = src_pos[:, 2] - col_start
    inside = (local_row >= 0) & (local_row < row_count) & (local_col >= 0) & (local_col < col_count)
    kept_amp = jnp.where(inside, src_amp, 0.0)
    safe_row = jnp.clip(local_row, 0, row_count - 1)
    safe_col = jnp.clip(local_col, 0, col_count - 1)
    source_grid = (
        jnp.zeros((LZ, row_count, col_count), jnp.float32)
        .at[src_pos[:, 0], safe_row, safe_col]
        .add(kept_amp)
    )
    electric, magnetic = (e_field, h_field)
    real_sum = jnp.zeros((NF, 4, row_count, col_count), jnp.float32)
    imag_sum = jnp.zeros((NF, 4, row_count, col_count), jnp.float32)
    for step_index in range(STEPS):
        moment = float(step_index + 1)
        row_e = shifted(electric[1:3, :, 0, :], "gx", -1)
        col_e = shifted(electric[0::2, :, :, 0], "gy", -1)
        magnetic = magnetic - courant * curl_forward(electric, row_e, col_e)
        row_h = shifted(magnetic[1:3, :, row_count - 1, :], "gx", 1)
        col_h = shifted(magnetic[0::2, :, :, col_count - 1], "gy", 1)
        electric = electric + update_scale * curl_backward(magnetic, row_h, col_h)
        electric = electric.at[2].add(math.sin(source_rate * moment) * source_grid)
        face_now = jnp.stack(
            [-magnetic[1, FACE], magnetic[0, FACE], electric[1, FACE], -electric[0, FACE]]
        )
        real_sum = real_sum + face_now[None] * jnp.cos(freqs * moment)[:, None, None, None]
        imag_sum = imag_sum + face_now[None] * jnp.sin(freqs * moment)[:, None, None, None]
    item_count = NF * 4
    currents = jnp.stack(
        [
            real_sum.reshape(item_count, row_count, col_count),
            imag_sum.reshape(item_count, row_count, col_count),
        ],
        1,
    ).astype(jnp.bfloat16)
    angle_index = jnp.arange(NA, dtype=jnp.int32)
    y_cells = col_start + jnp.arange(col_count, dtype=jnp.int32)
    y_real, y_imag = chirp(
        y_cells[:, None], (angle_index + NA // 4)[None, :], zoom_factor * grid_cols
    )
    y_table = jnp.concatenate([y_real, y_imag], 1).astype(jnp.bfloat16)
    flipped = jnp.swapaxes(currents, 2, 3)
    all_rows = jnp.arange(grid_rows, dtype=jnp.int32)
    x_real, x_imag = chirp(
        (angle_index - NA // 2)[None, :], all_rows[:, None], zoom_factor * grid_rows
    )
    x_table = jnp.concatenate([x_real, x_imag], 1).astype(jnp.bfloat16)
    product = jnp.einsum(
        "kbcx,xw->kbcw",
        lax.all_to_all(flipped, "gx", split_axis=2, concat_axis=3, tiled=True),
        x_table,
        preferred_element_type=jnp.float32,
    )
    part_re, part_im = complex_pair(
        product[:, 0, :, :NA], product[:, 0, :, NA:], product[:, 1, :, :NA], product[:, 1, :, NA:]
    )
    transformed = jnp.stack([part_re, part_im], 1).astype(jnp.bfloat16)
    sectioned = lax.all_to_all(transformed, "gx", split_axis=3, concat_axis=2, tiled=True)
    second = jnp.einsum("ibcu,cw->uibw", sectioned, y_table, preferred_element_type=jnp.float32)
    far_re, far_im = complex_pair(
        second[:, :, 0, :NA], second[:, :, 0, NA:], second[:, :, 1, :NA], second[:, :, 1, NA:]
    )
    partial_far = jnp.stack([far_re, far_im], 2)
    inv_norm = 1.0 / math.sqrt(grid_rows * grid_cols)
    far_field = lax.psum_scatter(partial_far, "gy", scatter_dimension=3, tiled=True) * inv_norm
    return (electric, magnetic, far_field)


def solution(mesh):
    placed = (
        P(None, None, "gx", "gy"),
        P(None, None, "gx", "gy"),
        P(None, "gx", "gy"),
        P(),
        P(),
        P(),
        P(),
    )
    return jax.shard_map(
        on_device,
        mesh=mesh,
        in_specs=placed,
        out_specs=(P(None, None, "gx", "gy"), P(None, None, "gx", "gy"), P("gx", None, None, "gy")),
        check_vma=False,
    )
```

profile of v0, /device:TPU:0, one launch (start us, length us, event | category | flops | bytes accessed | tf_op | source)
XLA Modules:
  0.0 507.8 jit_solution(7167283156874817417)
XLA Ops:
  19.7 7.1 %scatter_custom_fusion = f32[393216]{0:T(1024)} fusion(s32[1024]{0:T(1024)S(1)} %broadcast_select_fusion, f32[1024]{0:T(1024)S(1)} %broadcast_select_fusion.1, f32[]{:T(128)} %constant.104.clone.1), kind=kCustom, calls=%fused_computation.121 | custom fusion | flops 1024 | bytes 1572868
  33.3 6.3 %add_divide_fusion = f32[3,256,512]{2,1,0:T(8,128)S(1)} fusion(s32[3,256,512]{2,1,0:T(8,128)S(1)} %copy-done.32, f32[]{:T(128)} %bitcast.7, f32[]{:T(128)} %bitcast.6, f32[]{:T(128)} %bitcast.5, f32[]{:T(128)} %bitcast.4, f32[]{:T(128)} %bitcast.3, f32[]{:T(128)} %bitcast.2, f32[]{:T(128)} %bitcast.1, f32[]{:T(128)} %bitcast), kind=kLoop, calls=%fused_computation.101 | loop fusion | flops 9437184 | bytes 3145760 | tf_op jit(solution)/shard_map/div | solution.py:83
  47.0 4.4 slice_bitcast_fusion.10
  67.2 5.8 %collective-permute-start.2 = (f32[2,3,256]{2,0,1:T(2,128)S(1)}, f32[2,3,256]{2,0,1:T(2,128)S(1)}, u32[]{:S(2)}, u32[]{:S(2)}) collective-permute-start(f32[2,3,256]{2,0,1:T(2,128)S(1)} %bitcast.243), channel_id=1, source_target_pairs={{0,1},{1,2},{2,3},{4,5},{5,6},{6,7},{8,9},{9,10},{10,11},{12,13},{... | collective-permute-start | bytes 18440 | tf_op jit(solution)/shard_map/ppermute | solution.py:24
  77.4 4.3 slice_bitcast_fusion.7
  113.4 7.7 %mul.207 = f32[8,1,256,512]{2,1,0,3:T(1,128)} reshape(f32[2,4,256,512]{2,1,0,3:T(4,128)} %mul.206) | data formatting | bytes 8388608 | tf_op jit(solution)/shard_map/mul | solution.py:110
  142.2 4.7 collective-permute-start.6
  168.4 7.7 %mul.213 = f32[8,1,256,512]{2,1,0,3:T(1,128)} reshape(f32[2,4,256,512]{2,1,0,3:T(4,128)} %mul.212) | data formatting | bytes 8388608 | tf_op jit(solution)/shard_map/mul | solution.py:110
  176.1 10.6 %add_convert_fusion.1 = (bf16[8,1,256,512]{2,1,0,3:T(2,128)(2,1)S(1)}, bf16[8,1,256,512]{2,1,0,3:T(2,128)(2,1)S(1)}) fusion(f32[8,1,256,512]{2,1,0,3:T(1,128)} %mul.213, f32[8,1,256,512]{2,1,0,3:T(1,128)} %mul.207, f32[8]{0:T(128)S(1)} %copy-done.40, f32[8]{0:T(128)S(1)} %copy-done.37, f32[8]{0:T(128)S(1)} %copy-done.38, f32[8]{0:T(128)S(1)} %copy-done.39), kind=kLoop, calls=%fused_computation.30 | loop fusion | flops 8388608 | bytes 12583040 | tf_op jit(solution)/shard_map/convert.4
  186.7 10.5 %maximum_bitcast_fusion.2 = bf16[8,2,512,256]{3,1,0,2:T(2,128)(2,1)} fusion(bf16[8,1,256,512]{2,1,0,3:T(2,128)(2,1)S(1)} %get-tuple-element.47, bf16[8,1,256,512]{2,1,0,3:T(2,128)(2,1)S(1)} %get-tuple-element.46), kind=kLoop, calls=%fused_computation.28 | loop fusion | flops 8388608 | bytes 8388608 | tf_op jit(solution)/shard_map/transpose | solution.py:126
  197.2 6.1 %all-to-all-start = ((bf16[8,2,512,256]{3,1,0,2:T(2,128)(2,1)}), bf16[8,2,512,256]{3,1,0,2:T(2,128)(2,1)}, u32[]{:S(2)}, u32[]{:S(2)}) async-start(bf16[8,2,512,256]{3,1,0,2:T(2,128)(2,1)} %maximum_bitcast_fusion.2), calls=%async_computation | async-start | bytes 8388608 | tf_op jit(solution)/shard_map/all_to_all | solution.py:134
  203.3 35.0 %cosine_convert_fusion = (bf16[2048,1024]{1,0:T(8,128)(2,1)}, bf16[2048,1024]{1,0:T(8,128)(2,1)}) fusion(s32[1024]{0:T(1024)S(1)} %iota_add_fusion), kind=kLoop, calls=%fused_computation.13 | loop fusion | flops 35651584 | bytes 8392704 | tf_op jit(solution)/shard_map/convert.2
  238.4 14.1 %all-to-all-done = bf16[8,2,512,256]{3,1,0,2:T(2,128)(2,1)} async-done(((bf16[8,2,512,256]{3,1,0,2:T(2,128)(2,1)}), bf16[8,2,512,256]{3,1,0,2:T(2,128)(2,1)}, u32[]{:S(2)}, u32[]{:S(2)}) %all-to-all-start) | async-done | bytes 4194336 | tf_op jit(solution)/shard_map/all_to_all | solution.py:134
  259.6 8.8 %fusion.3 = f32[8,2,64,2048]{3,2,1,0:T(8,128)S(1)} fusion(bf16[8,2,64,2048]{3,2,1,0:T(8,128)(2,1)S(1)} %bitcast.236, bf16[2048,1024]{1,0:T(8,128)(2,1)S(1)} %copy-done.20, bf16[2048,1024]{1,0:T(8,128)(2,1)S(1)} %copy-done.19), kind=kOutput, calls=%fused_computation.8 | convolution fusion | flops 8606711808 | bytes 20971520 | tf_op jit(solution)/shard_map/kbcx,xw->kbcw/dot_general | solution.py:132
  269.4 7.8 %copy.114 = bf16[8,2,64,1024]{2,1,0,3:T(2,128)(2,1)} copy(bf16[8,2,64,1024]{3,2,1,0:T(8,128)(2,1)S(1)} %pad_maximum_fusion.3) | data formatting | bytes 4194304 | tf_op jit(solution)/shard_map/stack | solution.py:141
  277.2 7.6 %reshape.268 = bf16[8,2,65536]{2,1,0:T(2,128)(2,1)} reshape(bf16[1024,8,2,64]{3,2,1,0:T(2,128)(2,1)} %bitcast.229) | data formatting | bytes 4194304
  288.7 9.8 %cosine_convert_fusion.1 = (bf16[512,1024]{0,1:T(8,128)(2,1)S(1)}, bf16[512,1024]{0,1:T(8,128)(2,1)}) fusion(s32[1024]{0:T(1024)S(1)} %iota_add_fusion.1, s32[512]{0:T(512)S(1)} %iota_add_fusion.2), kind=kLoop, calls=%fused_computation.50 | loop fusion | flops 8912896 | bytes 2103296 | tf_op jit(solution)/shard_map/convert.6
  298.5 16.5 %all-to-all-done.1 = bf16[8,2,65536]{2,1,0:T(2,128)(2,1)S(1)} async-done(((bf16[8,2,65536]{2,1,0:T(2,128)(2,1)}), bf16[8,2,65536]{2,1,0:T(2,128)(2,1)S(1)}, u32[]{:S(2)}, u32[]{:S(2)}) %all-to-all-start.1) | async-done | bytes 2097184 | tf_op jit(solution)/shard_map/all_to_all | solution.py:142
  314.9 5.0 reshape.269
  320.0 9.2 %copy.115 = bf16[8,2,64,8,128]{4,2,3,1,0:T(8,128)(2,1)S(1)} copy(bf16[8,2,64,8,128]{2,1,0,4,3:T(2,128)(2,1)} %bitcast.230) | data formatting | bytes 4194304 | tf_op jit(solution)/shard_map/all_to_all | solution.py:142
  329.1 9.4 %convolution_bitcast_fusion = f32[128,8,2,2048]{0,3,2,1:T(8,128)} fusion(bf16[8,2,512,128]{3,2,1,0:T(8,128)(2,1)S(1)} %bitcast.237, bf16[512,1024]{0,1:T(8,128)(2,1)} %get-tuple-element.102, bf16[512,1024]{0,1:T(8,128)(2,1)S(1)} %get-tuple-element.101), kind=kOutput, calls=%fused_computation.17 | convolution fusion | flops 4299161600 | bytes 20971520 | tf_op jit(solution)/shard_map/ibcu,cw->uibw/dot_general | solution.py:143
  338.6 8.7 %slice_subtract_fusion = (f32[128,8,1,1024]{0,3,2,1:T(8,128)S(1)}, f32[128,8,1,1024]{0,3,2,1:T(8,128)}) fusion(f32[128,8,2,2048]{0,3,2,1:T(8,128)} %convolution_bitcast_fusion), kind=kLoop, calls=%fused_computation.27 | loop fusion | flops 2097152 | bytes 25165824 | tf_op jit(solution)/shard_map/sub | solution.py:68
  347.3 6.2 %pad_maximum_fusion = f32[128,8,2,1024]{0,3,2,1:T(8,128)} fusion(f32[128,8,1,1024]{0,3,2,1:T(8,128)} %get-tuple-element.43, f32[128,8,1,1024]{0,3,2,1:T(8,128)S(1)} %get-tuple-element.42), kind=kLoop, calls=%fused_computation.11 | loop fusion | flops 2097152 | bytes 16777216 | tf_op jit(solution)/shard_map/stack | solution.py:147
  353.5 143.1 %reduce-scatter.2.cloned.1.call-done = f32[128,8,2,256]{0,3,2,1:T(8,128)} async-done(((f32[128,8,2,1024]{0,3,2,1:T(8,128)}), f32[128,8,2,256]{0,3,2,1:T(8,128)}) %reduce-scatter.2.cloned.1.call-update) | async-done | bytes 2097168 | tf_op jit(solution)/shard_map/reduce_scatter | solution.py:149
  (247 shorter events, 136.1 us)
Async XLA Ops:
  7.2 5.0 copy-start.35
  8.1 38.9 %collective-permute-start.1 = (f32[2,3,512]{2,0,1:T(2,128)S(1)}, f32[2,3,512]{2,0,1:T(2,128)S(1)}, u32[]{:S(2)}, u32[]{:S(2)}) collective-permute-start(f32[2,3,512]{2,0,1:T(2,128)S(1)} %bitcast.238), channel_id=1, source_target_pairs={{4,0},{8,4},{12,8},{16,12},{20,16},{24,20},{28,24},{5,1},{9,5},{13... | collective-permute-start | bytes 36872 | tf_op jit(solution)/shard_map/ppermute | solution.py:24
  10.9 35.7 %collective-permute-start = (f32[2,3,256]{2,0,1:T(2,128)S(1)}, f32[2,3,256]{2,0,1:T(2,128)S(1)}, u32[]{:S(2)}, u32[]{:S(2)}) collective-permute-start(f32[2,3,256]{2,0,1:T(2,128)S(1)} %bitcast.241), channel_id=1, source_target_pairs={{1,0},{2,1},{3,2},{5,4},{6,5},{7,6},{9,8},{10,9},{11,10},{13,12},{... | collective-permute-start | bytes 18440 | tf_op jit(solution)/shard_map/ppermute | solution.py:24
  33.3 6.3 %copy-start.42 = (f32[2]{0:T(128)S(1)}, f32[2]{0:T(128)}, u32[]{:S(2)}) copy-start(f32[2]{0:T(128)} %param.17) | copy-start | bytes 28
  39.6 44.3 %copy-start.9 = (f32[3,256,512]{2,1,0:T(8,128)}, f32[3,256,512]{2,1,0:T(8,128)S(1)}, u32[]{:S(2)}) copy-start(f32[3,256,512]{2,1,0:T(8,128)S(1)} %add_divide_fusion) | copy-start | bytes 4718596
  47.0 5.2 %slice-start.8 = ((s8[4718592]{0:T(1024)(128)(4,1)}), s8[4194304]{0:T(1024)(128)(4,1)S(1)}, s32[]{:S(2)}) async-start(s8[4718592]{0:T(1024)(128)(4,1)} %bitcast.221), calls=%async_computation.12 | async-start | bytes 8388608
  47.0 5.2 %slice-start.9 = ((s8[4718592]{0:T(1024)(128)(4,1)}), s8[524288]{0:T(1024)(128)(4,1)S(1)}, s32[]{:S(2)}) async-start(s8[4718592]{0:T(1024)(128)(4,1)} %bitcast.221), calls=%async_computation.13 | async-start | bytes 1048576
  62.7 14.6 %collective-permute-start.3 = (f32[2,3,512]{2,0,1:T(2,128)S(1)}, f32[2,3,512]{2,0,1:T(2,128)S(1)}, u32[]{:S(2)}, u32[]{:S(2)}) collective-permute-start(f32[2,3,512]{2,0,1:T(2,128)S(1)} %bitcast.239), channel_id=1, source_target_pairs={{0,4},{4,8},{8,12},{12,16},{16,20},{20,24},{24,28},{1,5},{5,9},{9,... | collective-permute-start | bytes 36872 | tf_op jit(solution)/shard_map/ppermute | solution.py:24
  67.2 9.7 %collective-permute-start.2 = (f32[2,3,256]{2,0,1:T(2,128)S(1)}, f32[2,3,256]{2,0,1:T(2,128)S(1)}, u32[]{:S(2)}, u32[]{:S(2)}) collective-permute-start(f32[2,3,256]{2,0,1:T(2,128)S(1)} %bitcast.243), channel_id=1, source_target_pairs={{0,1},{1,2},{2,3},{4,5},{5,6},{6,7},{8,9},{9,10},{10,11},{12,13},{... | collective-permute-start | bytes 18440 | tf_op jit(solution)/shard_map/ppermute | solution.py:24
  77.4 5.2 %copy-start.24 = (f32[2,256,512]{2,1,0:T(8,128)S(1)}, f32[2,256,512]{2,1,0:T(8,128)}, u32[]{:S(2)}) copy-start(f32[2,256,512]{2,1,0:T(8,128)} %get-tuple-element.75) | copy-start | bytes 3145732
  86.1 6.8 %copy-start = (f32[3,3,256,512]{3,2,1,0:T(8,128)}, f32[3,3,256,512]{3,2,1,0:T(8,128)S(1)}, u32[]{:S(2)}) copy-start(f32[3,3,256,512]{3,2,1,0:T(8,128)S(1)} %get-tuple-element.51) | copy-start | bytes 14155780
  95.6 26.7 %collective-permute-start.5 = (f32[2,3,512]{2,0,1:T(2,128)}, f32[2,3,512]{2,0,1:T(2,128)S(1)}, u32[]{:S(2)}, u32[]{:S(2)}) collective-permute-start(f32[2,3,512]{2,0,1:T(2,128)} %bitcast.205), channel_id=1, source_target_pairs={{4,0},{8,4},{12,8},{16,12},{20,16},{24,20},{28,24},{5,1},{9,5},{13... | collective-permute-start | bytes 36872 | tf_op jit(solution)/shard_map/ppermute | solution.py:24
  98.3 22.9 %collective-permute-start.4 = (f32[2,3,256]{2,0,1:T(2,128)S(1)}, f32[2,3,256]{2,0,1:T(2,128)S(1)}, u32[]{:S(2)}, u32[]{:S(2)}) collective-permute-start(f32[2,3,256]{2,0,1:T(2,128)S(1)} %bitcast.242), channel_id=1, source_target_pairs={{1,0},{2,1},{3,2},{5,4},{6,5},{7,6},{9,8},{10,9},{11,10},{13,12},{... | collective-permute-start | bytes 18440 | tf_op jit(solution)/shard_map/ppermute | solution.py:24
  122.4 5.0 copy-start.17
  122.4 5.0 copy-start.33
  137.0 12.9 %collective-permute-start.7 = (f32[2,3,512]{2,0,1:T(2,128)S(1)}, f32[2,3,512]{2,0,1:T(2,128)S(1)}, u32[]{:S(2)}, u32[]{:S(2)}) collective-permute-start(f32[2,3,512]{2,0,1:T(2,128)S(1)} %bitcast.240), channel_id=1, source_target_pairs={{0,4},{4,8},{8,12},{12,16},{16,20},{20,24},{24,28},{1,5},{5,9},{9,... | collective-permute-start | bytes 36872 | tf_op jit(solution)/shard_map/ppermute | solution.py:24
  142.2 7.3 %collective-permute-start.6 = (f32[2,3,256]{2,0,1:T(2,128)S(1)}, f32[2,3,256]{2,0,1:T(2,128)S(1)}, u32[]{:S(2)}, u32[]{:S(2)}) collective-permute-start(f32[2,3,256]{2,0,1:T(2,128)S(1)} %bitcast.244), channel_id=1, source_target_pairs={{0,1},{1,2},{2,3},{4,5},{5,6},{6,7},{8,9},{9,10},{10,11},{12,13},{... | collective-permute-start | bytes 18440 | tf_op jit(solution)/shard_map/ppermute | solution.py:24
  168.3 7.7 %copy-start.37 = (f32[8]{0:T(128)S(1)}, f32[8]{0:T(128)}, u32[]{:S(2)}) copy-start(f32[8]{0:T(128)} %mul.209) | copy-start | bytes 100
  168.3 7.7 %copy-start.38 = (f32[8]{0:T(128)S(1)}, f32[8]{0:T(128)}, u32[]{:S(2)}) copy-start(f32[8]{0:T(128)} %mul.224) | copy-start | bytes 100
  168.3 7.7 %copy-start.39 = (f32[8]{0:T(128)S(1)}, f32[8]{0:T(128)}, u32[]{:S(2)}) copy-start(f32[8]{0:T(128)} %mul.220) | copy-start | bytes 100
  168.3 7.7 %copy-start.40 = (f32[8]{0:T(128)S(1)}, f32[8]{0:T(128)}, u32[]{:S(2)}) copy-start(f32[8]{0:T(128)} %mul.216) | copy-start | bytes 100
  197.2 55.2 %all-to-all-start = ((bf16[8,2,512,256]{3,1,0,2:T(2,128)(2,1)}), bf16[8,2,512,256]{3,1,0,2:T(2,128)(2,1)}, u32[]{:S(2)}, u32[]{:S(2)}) async-start(bf16[8,2,512,256]{3,1,0,2:T(2,128)(2,1)} %maximum_bitcast_fusion.2), calls=%async_computation | async-start | bytes 8388608 | tf_op jit(solution)/shard_map/all_to_all | solution.py:134
  284.8 30.2 %all-to-all-start.1 = ((bf16[8,2,65536]{2,1,0:T(2,128)(2,1)}), bf16[8,2,65536]{2,1,0:T(2,128)(2,1)S(1)}, u32[]{:S(2)}, u32[]{:S(2)}) async-start(bf16[8,2,65536]{2,1,0:T(2,128)(2,1)} %reshape.268), calls=%async_computation.1 | async-start | bytes 4194304 | tf_op jit(solution)/shard_map/all_to_all | solution.py:142
  288.4 208.3 %reduce-scatter.2.cloned.1.call-start = ((), (), s32[]{:S(2)}) async-start(), calls=%async_computation.3 | async-start | bytes 10485760 | tf_op jit(solution)/shard_map/reduce_scatter | solution.py:149
  (47 other events, 136.9 us)
Sparse Core Ops, SparseCore 0:
  353.6 142.9 reduce-scatter.1
where the time goes:
time: 518 us; the launch traced here: 508 us
  waiting for transfers between devices  174 us (34%)
  other arithmetic  137 us (26%)
  local copies, waits for them, and re-layouts  130 us (25%)
  starting transfers between devices  32.7 us (6%)
  matrix products  18.3 us (4%)
  between operations  15.2 us (3%)
    reduce_scatter x1, waiting for transfers between devices, on_device(): lax.psum_scatter(partial_far, 'gy', scatter_dimension=3, tiled=True)  143 us
    another operation x4, other arithmetic  56.2 us
    unnamed x125, local copies, waits for them, and re-layouts  29.4 us
    mul x8, local copies, waits for them, and re-layouts, on_device(): face_now[None] * jnp.cos(freqs * moment)[:, None, None, None]  23.7 us
    ppermute x8, starting transfers between devices, shifted(): return lax.ppermute(block, axis, route)  22.8 us
    all_to_all x1, waiting for transfers between devices, on_device(): lax.all_to_all(transformed, 'gx', split_axis=3, concat_axis=2, tiled=True)  16.5 us
    all_to_all x1, waiting for transfers between devices, on_device(): lax.all_to_all(flipped, 'gx', split_axis=2, concat_axis=3, tiled=True)  14.1 us
    transpose x1, other arithmetic, on_device(): flipped = jnp.swapaxes(currents, 2, 3)  10.5 us
  transfers between devices with their start and end apart: 11, of which 3 were waited for; matrix products, arithmetic and copies ran while one was open for 22% of the time, Pallas kernels for 0%

commit v1 on v0

v1 whole, which is shorter than its diff:
```python
import functools
import math

import jax
import jax.numpy as jnp
from jax import lax
from jax.experimental import pallas as pl
from jax.experimental.pallas import tpu as pltpu
from jax.sharding import PartitionSpec as P

LZ = 3
FACE = 1
STEPS = 2
NF = 2
NA = 1024
NMAT = 8

courant = 0.5
source_rate = 0.7
zoom_factor = 4

BASE = 32
CHUNK = 16
PAD = 128
ANY = pl.BlockSpec(memory_space=pl.ANY)
VM = pl.BlockSpec(memory_space=pltpu.VMEM)
SM = pl.BlockSpec(memory_space=pltpu.SMEM)
BIG = 60 * 1024 * 1024


def shifted(block, axis, distance):
    size = lax.axis_size(axis)
    route = [(i - distance, i) for i in range(size) if 0 <= i - distance < size]
    return lax.ppermute(block, axis, route)


def yee_kernel(
    grid_rows, grid_cols, parts,
    e_hbm, h_hbm, m_hbm, colf, colm, rowf, rowm, eps, pos, amp,
    e_out, h_out, sd_out,
    e_ext, h_ext, m_main, scale, src, first, sems,
):
    rows, cols = m_main.shape[1:]
    width = cols + PAD
    high = e_ext.shape[1]
    row0 = lax.axis_index("gx") * rows
    col0 = lax.axis_index("gy") * cols
    main_r = pl.ds(BASE, rows)
    copies = [
        pltpu.make_async_copy(e_hbm, e_ext.at[:, main_r, pl.ds(0, cols)], sems.at[0]),
        pltpu.make_async_copy(h_hbm, h_ext.at[:, main_r, pl.ds(0, cols)], sems.at[1]),
        pltpu.make_async_copy(m_hbm, m_main, sems.at[2]),
    ]
    for copy in copies:
        copy.start()
    count = amp.shape[1]
    step = min(count, 1024)
    used = high - 2 * CHUNK
    row_at = row0 + lax.broadcasted_iota(jnp.int32, (used, step), 0) + (CHUNK - BASE)
    lane = lax.broadcasted_iota(jnp.int32, (width, step), 0)
    col_at = col0 + jnp.where(lane < cols + PAD // 2, lane, lane - width)
    for start in range(0, count, step):
        at = pl.ds(start, step)
        amp_now = amp[:, at]
        hi = amp_now.astype(jnp.bfloat16).astype(jnp.float32)
        mid = (amp_now - hi).astype(jnp.bfloat16).astype(jnp.float32)
        low = amp_now - hi - mid
        hit_col = jnp.where(col_at == pos[2:3, at], 1.0, 0.0).astype(jnp.bfloat16)
        hit_row = row_at == pos[1:2, at]
        for layer in range(LZ):
            hit = hit_row & (pos[0:1, at] == layer)
            total = None
            for piece in (hi, mid, low):
                left = jnp.where(hit, piece, 0.0).astype(jnp.bfloat16)
                term = lax.dot_general(
                    left, hit_col, (((1,), (1,)), ((), ())), preferred_element_type=jnp.float32
                )
                total = term if total is None else total + term
            if start == 0:
                src[layer, CHUNK : CHUNK + used, :] = total
            else:
                src[layer, CHUNK : CHUNK + used, :] += total
    copies[2].wait()

    def scale_of(index, row, col):
        value = jnp.full(index.shape, eps[0], jnp.float32)
        for material in range(1, NMAT):
            value = jnp.where(index == material, eps[material], value)
        inside = (row >= 0) & (row < grid_rows) & (col >= 0) & (col < grid_cols)
        return jnp.where(inside, courant / value, 0.0)

    col_main = col0 + lax.broadcasted_iota(jnp.int32, (CHUNK, cols), 1)
    lane_pad = lax.broadcasted_iota(jnp.int32, (CHUNK, PAD), 1)
    col_pad = col0 + jnp.where(lane_pad < PAD // 2, cols + lane_pad, lane_pad - PAD)
    row_chunk = row0 + lax.broadcasted_iota(jnp.int32, (CHUNK, cols), 0)

    def fill(step_index, carry):
        r = pl.multiple_of(step_index * CHUNK, CHUNK)
        near = pl.ds(r, CHUNK)
        far = pl.ds(BASE + r, CHUNK)
        for layer in range(LZ):
            scale[layer, far, :cols] = scale_of(m_main[layer, near, :], row_chunk + r, col_main)
            scale[layer, far, cols:] = scale_of(
                colm[layer, near, :], row_chunk[:, :PAD] + r, col_pad
            )
        for plane in range(3 * LZ):
            e_ext[plane, far, cols:] = colf[plane, near, :]
            h_ext[plane, far, cols:] = colf[3 * LZ + plane, near, :]
        return carry

    lax.fori_loop(0, rows // CHUNK, fill, 0)
    lane_all = lax.broadcasted_iota(jnp.int32, (8, width), 1)
    col_all = col0 + jnp.where(lane_all < cols + PAD // 2, lane_all, lane_all - width)
    row_eight = row0 + lax.broadcasted_iota(jnp.int32, (8, width), 0)
    blank = jnp.zeros((8, width), jnp.float32)
    for place, target, offset, spare in (
        (0, BASE + rows, rows, BASE + rows + 8),
        (8, BASE - 8, -8, BASE - 16),
    ):
        for layer in range(LZ):
            scale[layer, target : target + 8, :] = scale_of(
                rowm[layer, place : place + 8, :], row_eight + offset, col_all
            )
            scale[layer, spare : spare + 8, :] = blank
        for plane in range(3 * LZ):
            e_ext[plane, target : target + 8, :] = rowf[plane, place : place + 8, :]
            h_ext[plane, target : target + 8, :] = rowf[3 * LZ + plane, place : place + 8, :]
            e_ext[plane, spare : spare + 8, :] = blank
            h_ext[plane, spare : spare + 8, :] = blank
    for plane in range(3 * LZ):
        e_ext[plane, high - 16 : high, :] = jnp.zeros((16, width), jnp.float32)
        h_ext[plane, 0:16, :] = jnp.zeros((16, width), jnp.float32)
    lane_c = lax.broadcasted_iota(jnp.int32, (CHUNK, width), 1)
    col_c = col0 + jnp.where(lane_c < cols + PAD // 2, lane_c, lane_c - width)
    weight = jnp.where(col_c >= 0, courant, 0.0)
    top = lax.axis_index("gx") == 0
    copies[0].wait()
    copies[1].wait()

    def magnetic_pass(index, carry):
        r = pl.multiple_of(index * CHUNK, CHUNK)
        now = pl.ds(r, CHUNK)
        more = pl.ds(r, CHUNK + 8)
        factor = weight * jnp.where(top & (index * CHUNK < BASE), 0.0, 1.0)
        zero = jnp.zeros((CHUNK, width), jnp.float32)
        ex = [e_ext[layer, now, :] for layer in range(LZ)] + [zero]
        ey = [e_ext[LZ + layer, now, :] for layer in range(LZ)] + [zero]
        for layer in range(LZ):
            ez = e_ext[2 * LZ + layer, now, :]
            ez_row = pltpu.roll(e_ext[2 * LZ + layer, more, :], CHUNK + 7, 0)[:CHUNK]
            ey_row = pltpu.roll(e_ext[LZ + layer, more, :], CHUNK + 7, 0)[:CHUNK]
            ez_col = pltpu.roll(ez, width - 1, 1)
            ex_col = pltpu.roll(ex[layer], width - 1, 1)
            curl_x = ez_col - ez - (ey[layer + 1] - ey[layer])
            curl_y = ex[layer + 1] - ex[layer] - (ez_row - ez)
            curl_z = ey_row - ey[layer] - (ex_col - ex[layer])
            for part, curl in enumerate((curl_x, curl_y, curl_z)):
                plane = part * LZ + layer
                h_ext[plane, now, :] = h_ext[plane, now, :] - factor * curl
        return carry

    def electric_pass(moment, last, index, carry):
        r = pl.multiple_of(index * CHUNK, CHUNK)
        now = pl.ds(r, CHUNK)
        more = pl.ds(pl.multiple_of(r - 8, 8), CHUNK + 8)
        drive = math.sin(source_rate * moment)
        zero = jnp.zeros((CHUNK, width), jnp.float32)
        hx = [zero] + [h_ext[layer, now, :] for layer in range(LZ)]
        hy = [zero] + [h_ext[LZ + layer, now, :] for layer in range(LZ)]
        for layer in range(LZ):
            hz = h_ext[2 * LZ + layer, now, :]
            hz_row = pltpu.roll(h_ext[2 * LZ + layer, more, :], 1, 0)[8:]
            hy_row = pltpu.roll(h_ext[LZ + layer, more, :], 1, 0)[8:]
            hx_now, hy_now = hx[layer + 1], hy[layer + 1]
            hz_col = pltpu.roll(hz, 1, 1)
            hx_col = pltpu.roll(hx_now, 1, 1)
            curl_x = hz - hz_col - (hy_now - hy[layer])
            curl_y = hx_now - hx[layer] - (hz - hz_row)
            curl_z = hy_now - hy_row - (hx_now - hx_col)
            factor = scale[layer, now, :]
            new_x = e_ext[layer, now, :] + factor * curl_x
            new_y = e_ext[LZ + layer, now, :] + factor * curl_y
            new_z = e_ext[2 * LZ + layer, now, :] + factor * curl_z + drive * src[layer, now, :]
            e_ext[layer, now, :] = new_x
            e_ext[LZ + layer, now, :] = new_y
            e_ext[2 * LZ + layer, now, :] = new_z
            if layer == FACE:
                faces = (-hy_now, hx_now, new_y, -new_x)
                for item, face in enumerate(faces):
                    if last:
                        old = first[item, now, :]
                        here = pl.ds(r - BASE, CHUNK)
                        span = cols // parts
                        for which, value in enumerate((old + face, face - old)):
                            value = value.astype(jnp.bfloat16)
                            for part in range(parts):
                                sd_out[item * parts + part, which, here, :] = value[
                                    :, part * span : (part + 1) * span
                                ]
                    else:
                        first[item, now, :] = face
        return carry

    chunks = high // CHUNK
    main0 = BASE // CHUNK
    main1 = main0 + rows // CHUNK
    lax.fori_loop(1, chunks - 1, magnetic_pass, 0)
    lax.fori_loop(1, chunks - 1, functools.partial(electric_pass, 1.0, False), 0)
    lax.fori_loop(1, main1, magnetic_pass, 0)
    out_h = pltpu.make_async_copy(h_ext.at[:, main_r, pl.ds(0, cols)], h_out, sems.at[3])
    out_h.start()
    lax.fori_loop(main0, main1, functools.partial(electric_pass, 2.0, True), 0)
    out_e = pltpu.make_async_copy(e_ext.at[:, main_r, pl.ds(0, cols)], e_out, sems.at[4])
    out_e.start()
    out_h.wait()
    out_e.wait()


def yee(e_field, h_field, material, eps_table, src_pos, src_amp):
    rows, cols = material.shape[1:]
    gx = lax.axis_size("gx")
    parts = gx // 4
    grid_rows = rows * gx
    grid_cols = cols * lax.axis_size("gy")
    planes = 3 * LZ
    e = e_field.reshape(planes, rows, cols)
    h = h_field.reshape(planes, rows, cols)
    mf = material.astype(jnp.float32)

    def edge(low, high, dim):
        cut = lambda a: lax.slice_in_dim(a, low, high, axis=dim)
        return jnp.concatenate([cut(e), cut(h), cut(mf)], 0)

    send_prev = jnp.swapaxes(edge(0, 2, 2), 1, 2)
    send_next = jnp.swapaxes(edge(cols - 2, cols, 2), 1, 2)
    right = shifted(send_prev, "gy", -1)
    left = shifted(send_next, "gy", 1)
    right = jnp.swapaxes(right, 1, 2)
    left = jnp.swapaxes(left, 1, 2)
    total = 2 * planes + LZ
    col_halo = jnp.concatenate(
        [right, jnp.zeros((total, rows, PAD - 4), jnp.float32), left], 2
    )
    send_up = jnp.concatenate([edge(0, 2, 1), col_halo[:, 0:2]], 2)
    send_down = jnp.concatenate([edge(rows - 2, rows, 1), col_halo[:, rows - 2 :]], 2)
    below = shifted(send_up, "gx", -1)
    above = shifted(send_down, "gx", 1)
    row_halo = jnp.concatenate(
        [below, jnp.zeros((total, 12, cols + PAD), jnp.float32), above], 1
    )
    colf, colm = col_halo[: 2 * planes], col_halo[2 * planes :].astype(jnp.int32)
    rowf, rowm = row_halo[: 2 * planes], row_halo[2 * planes :].astype(jnp.int32)
    high = rows + 2 * BASE
    width = cols + PAD
    f32 = jnp.float32
    out = pl.pallas_call(
        functools.partial(yee_kernel, grid_rows, grid_cols, parts),
        out_shape=(
            jax.ShapeDtypeStruct((planes, rows, cols), f32),
            jax.ShapeDtypeStruct((planes, rows, cols), f32),
            jax.ShapeDtypeStruct((gx, 2, rows, cols // parts), jnp.bfloat16),
        ),
        in_specs=[ANY, ANY, ANY, VM, VM, VM, VM, SM, VM, VM],
        out_specs=(ANY, ANY, VM),
        scratch_shapes=[
            pltpu.VMEM((planes, high, width), f32),
            pltpu.VMEM((planes, high, width), f32),
            pltpu.VMEM((LZ, rows, cols), jnp.int32),
            pltpu.VMEM((LZ, high, width), f32),
            pltpu.VMEM((LZ, high, width), f32),
            pltpu.VMEM((4, high, width), f32),
            pltpu.SemaphoreType.DMA((5,)),
        ],
        compiler_params=pltpu.CompilerParams(vmem_limit_bytes=BIG),
        name="yee",
    )(
        e, h, material, colf, colm, rowf, rowm,
        eps_table, jnp.swapaxes(src_pos, 0, 1), src_amp[None, :],
    )
    return out


def table_kernel(a_re, a_im, b_re, b_im, out):
    lo_re, lo_im = b_re[...], b_im[...]
    for block in range(a_re.shape[1]):
        hi_re = a_re[:, block : block + 1]
        hi_im = a_im[:, block : block + 1]
        at = slice(block * 128, block * 128 + 128)
        out[0, 0, :, at] = (hi_re * lo_re - hi_im * lo_im).astype(jnp.bfloat16)
        out[0, 1, :, at] = (hi_re * lo_im + hi_im * lo_re).astype(jnp.bfloat16)


def unit(phase, period):
    angle = jnp.remainder(phase, period).astype(jnp.float32) * (2.0 * math.pi / period)
    return jnp.cos(angle), -jnp.sin(angle)


def table(row_index, first, length, period, blocks):
    count = row_index.shape[0]
    high = first + 128 * jnp.arange(length // 128, dtype=jnp.int32)
    low = jnp.arange(128, dtype=jnp.int32)
    a_re, a_im = unit(row_index[:, None] * high[None, :], period)
    b_re, b_im = unit(row_index[:, None] * low[None, :], period)
    size = count // blocks
    one = pl.BlockSpec((size, length // 128), lambda i: (i, 0))
    two = pl.BlockSpec((size, 128), lambda i: (i, 0))
    return pl.pallas_call(
        table_kernel,
        grid=(blocks,),
        out_shape=jax.ShapeDtypeStruct((blocks, 2, size, length), jnp.bfloat16),
        in_specs=[one, one, two, two],
        out_specs=pl.BlockSpec((1, 2, size, length), lambda i: (i, 0, 0, 0)),
        cost_estimate=pl.CostEstimate(
            flops=8 * count * length, bytes_accessed=4 * count * length, transcendentals=0
        ),
        name="chirp",
    )(a_re, a_im, b_re, b_im)


def rows_kernel(mix, tab, v, out):
    nu = tab.shape[2]
    span = v.shape[3]
    left = tab[0].reshape(2 * nu, tab.shape[3])
    got = []
    for which in range(2):
        right = v[:, which].reshape(-1, span)
        both = jnp.dot(left, right, preferred_element_type=jnp.float32)
        got.append((both[:nu], both[nu:]))
    (s_re, s_im), (d_re, d_im) = got
    for f in range(NF):
        p_re, p_im, q_re, q_im = (mix[f, i] for i in range(4))
        re = p_re * s_re - p_im * s_im + (q_re * d_re - q_im * d_im)
        im = p_re * s_im + p_im * s_re + (q_re * d_im + q_im * d_re)
        out[0, f, 0] = re.astype(jnp.bfloat16)
        out[0, f, 1] = im.astype(jnp.bfloat16)


def cols_kernel(g, tab, out):
    parts, span = g.shape[1], g.shape[5]
    width = tab.shape[2]
    shares = out.shape[0]
    vb = out.shape[4]
    y_re = tab[0, 0]
    y_im = tab[0, 1]
    g_re = jnp.concatenate([g[0, p, 0, 0] for p in range(parts)], 1)
    g_im = jnp.concatenate([g[0, p, 0, 1] for p in range(parts)], 1)
    dot = functools.partial(jnp.dot, preferred_element_type=jnp.float32)
    re = dot(g_re, y_re) - dot(g_im, y_im)
    im = dot(g_re, y_im) + dot(g_im, y_re)
    for share in range(shares):
        out[share, 0, 0] = re[:, share * vb : (share + 1) * vb].astype(out.dtype)
        out[share, 0, 1] = im[:, share * vb : (share + 1) * vb].astype(out.dtype)


def on_device(e_field, h_field, material, eps_table, src_pos, src_amp, freqs):
    rows, cols = material.shape[1:]
    gx, gy = lax.axis_size("gx"), lax.axis_size("gy")
    grid_rows, grid_cols = rows * gx, cols * gy
    parts = gx // 4
    span = cols // parts
    nu = NA // gx
    vb = NA // gy
    col_start = lax.axis_index("gy") * cols
    bf16 = jnp.bfloat16
    angle_index = jnp.arange(NA, dtype=jnp.int32)
    x_tab = table(angle_index - NA // 2, 0, grid_rows, zoom_factor * grid_rows, gx)
    y_cells = col_start + jnp.arange(cols, dtype=jnp.int32)
    y_tab = table(y_cells, NA // 4, NA, zoom_factor * grid_cols, 1)
    e_new, h_new, sd = yee(e_field, h_field, material, eps_table, src_pos, src_amp)
    got = lax.all_to_all(sd, "gx", split_axis=0, concat_axis=0, tiled=True)
    turn_re, turn_im = jnp.cos(1.5 * freqs), jnp.sin(1.5 * freqs)
    half_re, half_im = jnp.cos(0.5 * freqs), jnp.sin(0.5 * freqs)
    mix = jnp.stack(
        [turn_re * half_re, turn_im * half_re, -turn_im * half_im, turn_re * half_im], 1
    )
    g = pl.pallas_call(
        rows_kernel,
        grid=(gx,),
        out_shape=jax.ShapeDtypeStruct((gx, NF, 2, nu, span), bf16),
        in_specs=[
            SM,
            pl.BlockSpec((1, 2, nu, grid_rows), lambda i: (i, 0, 0, 0)),
            pl.BlockSpec((gx, 2, rows, span), lambda i: (0, 0, 0, 0)),
        ],
        out_specs=pl.BlockSpec((1, NF, 2, nu, span), lambda i: (i, 0, 0, 0, 0)),
        compiler_params=pltpu.CompilerParams(vmem_limit_bytes=BIG),
        name="rows",
    )(mix, x_tab, got)
    moved = lax.all_to_all(g, "gx", split_axis=0, concat_axis=0, tiled=True)
    moved = moved.reshape(4, parts, NF, 2, nu, span)
    share = pl.pallas_call(
        cols_kernel,
        grid=(NF, 4),
        out_shape=jax.ShapeDtypeStruct((gy, NF * 4, 2, nu, vb), bf16),
        in_specs=[
            pl.BlockSpec((1, parts, 1, 2, nu, span), lambda f, k: (k, 0, f, 0, 0, 0)),
            pl.BlockSpec((1, 2, cols, NA), lambda f, k: (0, 0, 0, 0)),
        ],
        out_specs=pl.BlockSpec((gy, 1, 2, nu, vb), lambda f, k: (0, f * 4 + k, 0, 0, 0)),
        compiler_params=pltpu.CompilerParams(vmem_limit_bytes=BIG),
        name="cols",
    )(moved, y_tab)
    inv_norm = 1.0 / math.sqrt(grid_rows * grid_cols)
    summed = lax.psum_scatter(share, "gy", scatter_dimension=0, tiled=True)
    far = jnp.transpose(summed[0].astype(jnp.float32) * inv_norm, (2, 0, 1, 3))
    shape = e_field.shape
    return (e_new.reshape(shape), h_new.reshape(shape), far)


def solution(mesh):
    placed = (
        P(None, None, "gx", "gy"),
        P(None, None, "gx", "gy"),
        P(None, "gx", "gy"),
        P(),
        P(),
        P(),
        P(),
    )
    return jax.shard_map(
        on_device,
        mesh=mesh,
        in_specs=placed,
        out_specs=(P(None, None, "gx", "gy"), P(None, None, "gx", "gy"), P("gx", None, None, "gy")),
        check_vma=False,
    )
```

time: 518 us -> 236 us (0.46); the launches traced: 508 us -> 235 us
  other arithmetic: 137 us -> 16.4 us
  local copies, waits for them, and re-layouts: 130 us -> 24.1 us
  waiting for transfers between devices: 174 us -> 104 us
  Pallas kernels: 0 us -> 55.5 us
  matrix products: 18.3 us -> 0 us
  starting transfers between devices: 32.7 us -> 20.5 us
    another operation x14 -> x2, other arithmetic: 74.1 us -> 0.71 us  [on_device(): jnp.stack([turn_re * half_re, turn_im * half_re, -turn_im * half_im, turn...]
    reduce_scatter x1, waiting for transfers between devices: 143 us -> 75.4 us  [on_device(): summed = lax.psum_scatter(share, 'gy', scatter_dimension=0, tiled=True)]
    pallas_call x0 -> x5, Pallas kernels: none -> 55.5 us  [the longest x1 21.7 us: yee(): pl.pallas_call(functools.partial(yee_kernel, grid_rows, grid_cols, parts)...]
    mul x12 -> x0, local copies, waits for them, and re-layouts: 25.1 us -> none  [the longest x8 23.7 us: on_device(): face_now[None] * jnp.cos(freqs * moment)[:, None, None, None]]
    unnamed x125 -> x13, local copies, waits for them, and re-layouts: 29.4 us -> 6.73 us
    dot_general x2 -> x0, matrix products: 18.3 us -> none  [the longest x1 9.44 us: on_device(): jnp.einsum('ibcu,cw->uibw', sectioned, y_table, preferred_element_type=jn...]
    another operation x17 -> x4, local copies, waits for them, and re-layouts: 18.3 us -> 0.37 us  [on_device(): jnp.stack([turn_re * half_re, turn_im * half_re, -turn_im * half_im, turn...]
    sub x4 -> x0, other arithmetic: 15.5 us -> none  [the longest x1 8.72 us: complex_pair(): return (product_re_re - product_im_im, product_re_im + product_im_re)]
  transfers between devices with their start and end apart: 11 -> 7, of which waited for: 3 -> 3; matrix products, arithmetic and copies ran while one was open for 22% -> 7% of each run, Pallas kernels for 0% -> 6%
where the time goes in v1:
time: 236 us; the launch traced here: 235 us
  waiting for transfers between devices  104 us (44%)
  Pallas kernels  55.5 us (24%)
  local copies, waits for them, and re-layouts  24.1 us (10%)
  starting transfers between devices  20.5 us (9%)
  other arithmetic  16.4 us (7%)
  between operations  14.3 us (6%)
    reduce_scatter x1, waiting for transfers between devices, on_device(): summed = lax.psum_scatter(share, 'gy', scatter_dimension=0, tiled=True)  75.4 us
    pallas_call x1, Pallas kernels, yee(): pl.pallas_call(functools.partial(yee_kernel, grid_rows, grid_cols, parts)...  21.7 us
    all_to_all x1, waiting for transfers between devices, on_device(): moved = lax.all_to_all(g, 'gx', split_axis=0, concat_axis=0, tiled=True)  18.8 us
    pallas_call x2, Pallas kernels, table(): pl.pallas_call(table_kernel, grid=(blocks,), out_shape=jax.ShapeDtypeStru...  13.1 us
    ppermute x4, starting transfers between devices, shifted(): return lax.ppermute(block, axis, route)  11.2 us
    pallas_call x1, Pallas kernels, on_device(): pl.pallas_call(rows_kernel, grid=(gx,), out_shape=jax.ShapeDtypeStruct((g...  10.9 us
    slice x11, local copies, waits for them, and re-layouts, edge(): cut = lambda a: lax.slice_in_dim(a, low, high, axis=dim)  10.8 us
    all_to_all x1, waiting for transfers between devices, on_device(): got = lax.all_to_all(sd, 'gx', split_axis=0, concat_axis=0, tiled=True)  9.89 us
  transfers between devices with their start and end apart: 7, of which 3 were waited for; matrix products, arithmetic and copies ran while one was open for 7% of the time, Pallas kernels for 6%

profile of v1, /device:TPU:0, one launch (start us, length us, event | category | flops | bytes accessed | tf_op | source)
XLA Modules:
  0.0 235.0 jit_solution(13529793747747901945)
XLA Ops:
  7.2 2.0 fusion.20
  9.6 3.6 %fusion.21 = (f32[9,256,2]{2,1,0:T(8,128)}, f32[9,256,2]{2,1,0:T(8,128)}) fusion(f32[9,256,512]{2,1,0:T(8,128)} %bitcast.30), kind=kLoop, calls=%fused_computation.65 | loop fusion | bytes 73728 | tf_op jit(solution)/shard_map/slice | solution.py:231
  13.1 1.6 copy.29
  18.7 5.6 %collective-permute-start.1 = (f32[21,2,256]{2,1,0:T(2,128)S(1)}, f32[21,2,256]{2,1,0:T(2,128)S(1)}, u32[]{:S(2)}, u32[]{:S(2)}) collective-permute-start(f32[21,2,256]{2,1,0:T(2,128)S(1)} %maximum_bitcast_fusion.1), channel_id=1, source_target_pairs={{0,1},{1,2},{2,3},{4,5},{5,6},{6,7},{8,9},{9,10},{10,11},{12,13},{... | collective-permute-start | bytes 129032 | tf_op jit(solution)/shard_map/ppermute | solution.py:34
  27.3 2.4 %copy.35 = f32[21,2,256]{1,2,0:T(8,128)} copy(f32[21,2,256]{2,1,0:T(2,128)S(1)} %collective-permute-done.1) | data formatting | bytes 86016 | tf_op jit(solution)/shard_map/ppermute | solution.py:34
  29.7 2.6 %pad_maximum_fusion = f32[21,256,128]{2,1,0:T(8,128)S(1)} fusion(f32[21,256,2]{2,1,0:T(8,128)} %bitcast.26, f32[21,256,2]{2,1,0:T(8,128)S(1)} %bitcast.25, f32[128]{0:T(128)S(1)} %pad.16.clone), kind=kLoop, calls=%fused_computation | loop fusion | flops 1376256 | bytes 2839040 | tf_op jit(solution)/shard_map/concatenate | solution.py:241
  33.7 3.0 %collective-permute-start.3 = (f32[21,2,640]{2,1,0:T(2,128)S(1)}, f32[21,2,640]{2,1,0:T(2,128)S(1)}, u32[]{:S(2)}, u32[]{:S(2)}) collective-permute-start(f32[21,2,640]{2,1,0:T(2,128)S(1)} %pad_maximum_fusion.3), channel_id=1, source_target_pairs={{0,4},{4,8},{8,12},{12,16},{16,20},{20,24},{24,28},{1,5},{5,9},{9,... | collective-permute-start | bytes 322568 | tf_op jit(solution)/shard_map/ppermute | solution.py:34
  37.5 1.6 slice.78.colf
  40.8 21.7 %yee.1 = (f32[9,256,512]{2,1,0:T(8,128)}, f32[9,256,512]{2,1,0:T(8,128)}, bf16[8,2,256,256]{3,2,1,0:T(8,128)(2,1)}) custom-call(f32[9,256,512]{2,1,0:T(8,128)} %bitcast.29, f32[9,256,512]{2,1,0:T(8,128)} %bitcast.32, s32[3,256,512]{2,1,0:T(8,128)} %m_hbm.1, f32[18,256,128]{2,1,0:T(8,128)} %slice.78.colf, s32[3,256,128]{2,1,0:T(8,128)} %slice_convert_fusion.colm, ...), custom_call_target="tpu_custom_call" | custom-call | tf_op jit(solution)/shard_map/yee/pallas_call | solution.py:256
  62.5 5.7 %all-to-all-start = ((bf16[8,2,256,256]{3,2,1,0:T(8,128)(2,1)}), bf16[8,2,256,256]{3,2,1,0:T(8,128)(2,1)S(1)}, u32[]{:S(2)}, u32[]{:S(2)}) async-start(bf16[8,2,256,256]{3,2,1,0:T(8,128)(2,1)} %get-tuple-element.8), calls=%async_computation | async-start | bytes 4194304 | tf_op jit(solution)/shard_map/all_to_all | solution.py:370
  69.0 3.3 %sine_negate_fusion = (f32[1024,128]{1,0:T(8,128)}, f32[1024,128]{1,0:T(8,128)}) fusion(s32[1024]{0:T(1024)S(1)} %iota_add_fusion), kind=kLoop, calls=%fused_computation.9 | loop fusion | flops 1966080 | bytes 1052672 | tf_op jit(solution)/shard_map/neg | solution.py:295
  72.2 2.8 %sine_negate_fusion.1 = (f32[1024,16]{1,0:T(8,128)}, f32[1024,16]{1,0:T(8,128)}) fusion(f32[1024,16]{1,0:T(8,128)S(1)} %copy.40), kind=kLoop, calls=%fused_computation.12 | loop fusion | flops 32768 | bytes 196608 | tf_op jit(solution)/shard_map/neg | solution.py:295
  75.0 9.3 %chirp.2.tab = bf16[8,2,128,2048]{3,2,1,0:T(8,128)(2,1)} custom-call(f32[1024,16]{1,0:T(8,128)} %get-tuple-element.33.a_re, f32[1024,16]{1,0:T(8,128)} %get-tuple-element.32.a_im, f32[1024,128]{1,0:T(8,128)} %get-tuple-element.37.b_re, f32[1024,128]{1,0:T(8,128)} %get-tuple-element.36.b_im), custom_call_target="tpu_custom_call" | custom-call | flops 16777216 | bytes 8388608 | tf_op jit(solution)/shard_map/chirp/pallas_call | solution.py:307
  85.0 9.9 %all-to-all-done.v = bf16[8,2,256,256]{3,2,1,0:T(8,128)(2,1)S(1)} async-done(((bf16[8,2,256,256]{3,2,1,0:T(8,128)(2,1)}), bf16[8,2,256,256]{3,2,1,0:T(8,128)(2,1)S(1)}, u32[]{:S(2)}, u32[]{:S(2)}) %all-to-all-start) | async-done | bytes 2097184 | tf_op jit(solution)/shard_map/all_to_all | solution.py:370
  96.2 10.9 %rows.1 = bf16[8,2,2,128,256]{4,3,2,1,0:T(8,128)(2,1)} custom-call(f32[2,4]{1,0:T(2,128)} %pad_maximum_fusion.4.mix, bf16[8,2,128,2048]{3,2,1,0:T(8,128)(2,1)} %chirp.2.tab, bf16[8,2,256,256]{3,2,1,0:T(8,128)(2,1)} %copy-done), custom_call_target="tpu_custom_call" | custom-call | tf_op jit(solution)/shard_map/rows/pallas_call | solution.py:376
  107.1 3.6 %all-to-all-start.1 = ((bf16[8,2,2,128,256]{4,3,2,1,0:T(8,128)(2,1)}), bf16[8,2,2,128,256]{4,3,2,1,0:T(8,128)(2,1)S(1)}, u32[]{:S(2)}, u32[]{:S(2)}) async-start(bf16[8,2,2,128,256]{4,3,2,1,0:T(8,128)(2,1)} %rows.1), calls=%async_computation.1 | async-start | bytes 4194304 | tf_op jit(solution)/shard_map/all_to_all | solution.py:389
  111.0 1.9 sine_negate_fusion.2
  113.0 1.7 sine_negate_fusion.3
  114.6 3.8 %chirp.3.tab = bf16[1,2,512,1024]{3,2,1,0:T(8,128)(2,1)} custom-call(f32[512,8]{1,0:T(8,128)} %get-tuple-element.35.a_re, f32[512,8]{1,0:T(8,128)} %get-tuple-element.34.a_im, f32[512,128]{1,0:T(8,128)} %get-tuple-element.39.b_re, f32[512,128]{1,0:T(8,128)} %get-tuple-element.38.b_im), custom_call_target="tpu_custom_call" | custom-call | flops 4194304 | bytes 2097152 | tf_op jit(solution)/shard_map/chirp/pallas_call | solution.py:307
  118.5 18.8 %all-to-all-done.1 = bf16[8,2,2,128,256]{4,3,2,1,0:T(8,128)(2,1)S(1)} async-done(((bf16[8,2,2,128,256]{4,3,2,1,0:T(8,128)(2,1)}), bf16[8,2,2,128,256]{4,3,2,1,0:T(8,128)(2,1)S(1)}, u32[]{:S(2)}, u32[]{:S(2)}) %all-to-all-start.1) | async-done | bytes 2097184 | tf_op jit(solution)/shard_map/all_to_all | solution.py:389
  138.6 9.7 %cols.1 = bf16[4,8,2,128,256]{4,3,2,1,0:T(8,128)(2,1)} custom-call(bf16[4,2,2,2,128,256]{5,4,3,2,1,0:T(8,128)(2,1)} %bitcast.33, bf16[1,2,512,1024]{3,2,1,0:T(8,128)(2,1)} %chirp.3.tab), custom_call_target="tpu_custom_call" | custom-call | tf_op jit(solution)/shard_map/cols/pallas_call | solution.py:391
  148.4 75.4 %reduce-scatter.2.cloned.1.call-done = bf16[1,8,2,128,256]{4,3,2,1,0:T(8,128)(2,1)} async-done(((bf16[4,8,2,128,256]{4,3,2,1,0:T(8,128)(2,1)}), bf16[1,8,2,128,256]{4,3,2,1,0:T(8,128)(2,1)}) %reduce-scatter.2.cloned.1.call-update) | async-done | bytes 1048592 | tf_op jit(solution)/shard_map/reduce_scatter | solution.py:404
  223.8 1.4 multiply_bitcast_fusion
  225.2 2.9 %copy.42 = f32[128,8,2,256]{3,2,1,0:T(2,128)} copy(f32[128,8,2,256]{3,0,2,1:T(8,128)S(1)} %multiply_bitcast_fusion) | data formatting | bytes 4194304
  (57 shorter events, 15.5 us)
Async XLA Ops:
  9.6 5.2 %copy-start.2 = (s32[3,256,512]{2,1,0:T(8,128)S(1)}, s32[3,256,512]{2,1,0:T(8,128)}, u32[]{:S(2)}) copy-start(s32[3,256,512]{2,1,0:T(8,128)} %m_hbm.1) | copy-start | bytes 4718596
  15.0 1.1 copy-start.4
  16.1 2.0 copy-start.3
  16.5 10.0 %collective-permute-start = (f32[21,2,256]{2,1,0:T(2,128)S(1)}, f32[21,2,256]{2,1,0:T(2,128)S(1)}, u32[]{:S(2)}, u32[]{:S(2)}) collective-permute-start(f32[21,2,256]{2,1,0:T(2,128)S(1)} %maximum_bitcast_fusion), channel_id=1, source_target_pairs={{1,0},{2,1},{3,2},{5,4},{6,5},{7,6},{9,8},{10,9},{11,10},{13,12},{... | collective-permute-start | bytes 129032 | tf_op jit(solution)/shard_map/ppermute | solution.py:34
  18.7 8.6 %collective-permute-start.1 = (f32[21,2,256]{2,1,0:T(2,128)S(1)}, f32[21,2,256]{2,1,0:T(2,128)S(1)}, u32[]{:S(2)}, u32[]{:S(2)}) collective-permute-start(f32[21,2,256]{2,1,0:T(2,128)S(1)} %maximum_bitcast_fusion.1), channel_id=1, source_target_pairs={{0,1},{1,2},{2,3},{4,5},{5,6},{6,7},{8,9},{9,10},{10,11},{12,13},{... | collective-permute-start | bytes 129032 | tf_op jit(solution)/shard_map/ppermute | solution.py:34
  32.4 6.8 %collective-permute-start.2 = (f32[21,2,640]{2,1,0:T(2,128)S(1)}, f32[21,2,640]{2,1,0:T(2,128)S(1)}, u32[]{:S(2)}, u32[]{:S(2)}) collective-permute-start(f32[21,2,640]{2,1,0:T(2,128)S(1)} %pad_maximum_fusion.2), channel_id=1, source_target_pairs={{4,0},{8,4},{12,8},{16,12},{20,16},{24,20},{28,24},{5,1},{9,5},{13... | collective-permute-start | bytes 322568 | tf_op jit(solution)/shard_map/ppermute | solution.py:34
  33.7 5.4 %collective-permute-start.3 = (f32[21,2,640]{2,1,0:T(2,128)S(1)}, f32[21,2,640]{2,1,0:T(2,128)S(1)}, u32[]{:S(2)}, u32[]{:S(2)}) collective-permute-start(f32[21,2,640]{2,1,0:T(2,128)S(1)} %pad_maximum_fusion.3), channel_id=1, source_target_pairs={{0,4},{4,8},{8,12},{12,16},{16,20},{20,24},{24,28},{1,5},{5,9},{9,... | collective-permute-start | bytes 322568 | tf_op jit(solution)/shard_map/ppermute | solution.py:34
  62.5 5.7 %copy-start.5 = (f32[2]{0:T(128)S(1)}, f32[2]{0:T(128)}, u32[]{:S(2)}) copy-start(f32[2]{0:T(128)} %param.13) | copy-start | bytes 28
  62.5 32.3 %all-to-all-start = ((bf16[8,2,256,256]{3,2,1,0:T(8,128)(2,1)}), bf16[8,2,256,256]{3,2,1,0:T(8,128)(2,1)S(1)}, u32[]{:S(2)}, u32[]{:S(2)}) async-start(bf16[8,2,256,256]{3,2,1,0:T(8,128)(2,1)} %get-tuple-element.8), calls=%async_computation | async-start | bytes 4194304 | tf_op jit(solution)/shard_map/all_to_all | solution.py:370
  94.8 1.3 copy-start
  107.1 30.2 %all-to-all-start.1 = ((bf16[8,2,2,128,256]{4,3,2,1,0:T(8,128)(2,1)}), bf16[8,2,2,128,256]{4,3,2,1,0:T(8,128)(2,1)S(1)}, u32[]{:S(2)}, u32[]{:S(2)}) async-start(bf16[8,2,2,128,256]{4,3,2,1,0:T(8,128)(2,1)} %rows.1), calls=%async_computation.1 | async-start | bytes 4194304 | tf_op jit(solution)/shard_map/all_to_all | solution.py:389
  110.7 113.1 %reduce-scatter.2.cloned.1.call-start = ((), (), s32[]{:S(2)}) async-start(), calls=%async_computation.3 | async-start | bytes 5242880 | tf_op jit(solution)/shard_map/reduce_scatter | solution.py:404
  137.3 1.3 copy-start.1
Sparse Core Ops, SparseCore 0:
  148.5 75.2 reduce-scatter.1

commit v2 on v1

--- a/solution.py
+++ b/solution.py
@@ -36,7 +36,7 @@
 
 def yee_kernel(
     grid_rows, grid_cols, parts,
-    e_hbm, h_hbm, m_hbm, colf, colm, rowf, rowm, eps, pos, amp,
+    e_hbm, h_hbm, m_hbm, colh, rowh, eps, pos, amp,
     e_out, h_out, sd_out,
     e_ext, h_ext, m_main, scale, src, first, sems,
 ):
@@ -101,11 +101,11 @@
         for layer in range(LZ):
             scale[layer, far, :cols] = scale_of(m_main[layer, near, :], row_chunk + r, col_main)
             scale[layer, far, cols:] = scale_of(
-                colm[layer, near, :], row_chunk[:, :PAD] + r, col_pad
+                colh[6 * LZ + layer, near, :], row_chunk[:, :PAD] + r, col_pad
             )
         for plane in range(3 * LZ):
-            e_ext[plane, far, cols:] = colf[plane, near, :]
-            h_ext[plane, far, cols:] = colf[3 * LZ + plane, near, :]
+            e_ext[plane, far, cols:] = colh[plane, near, :]
+            h_ext[plane, far, cols:] = colh[3 * LZ + plane, near, :]
         return carry
 
     lax.fori_loop(0, rows // CHUNK, fill, 0)
@@ -119,12 +119,12 @@
     ):
         for layer in range(LZ):
             scale[layer, target : target + 8, :] = scale_of(
-                rowm[layer, place : place + 8, :], row_eight + offset, col_all
+                rowh[6 * LZ + layer, place : place + 8, :], row_eight + offset, col_all
             )
             scale[layer, spare : spare + 8, :] = blank
         for plane in range(3 * LZ):
-            e_ext[plane, target : target + 8, :] = rowf[plane, place : place + 8, :]
-            h_ext[plane, target : target + 8, :] = rowf[3 * LZ + plane, place : place + 8, :]
+            e_ext[plane, target : target + 8, :] = rowh[plane, place : place + 8, :]
+            h_ext[plane, target : target + 8, :] = rowh[3 * LZ + plane, place : place + 8, :]
             e_ext[plane, spare : spare + 8, :] = blank
             h_ext[plane, spare : spare + 8, :] = blank
     for plane in range(3 * LZ):
@@ -225,11 +225,10 @@
     planes = 3 * LZ
     e = e_field.reshape(planes, rows, cols)
     h = h_field.reshape(planes, rows, cols)
-    mf = material.astype(jnp.float32)
 
     def edge(low, high, dim):
         cut = lambda a: lax.slice_in_dim(a, low, high, axis=dim)
-        return jnp.concatenate([cut(e), cut(h), cut(mf)], 0)
+        return jnp.concatenate([cut(e), cut(h), cut(material).astype(jnp.float32)], 0)
 
     send_prev = jnp.swapaxes(edge(0, 2, 2), 1, 2)
     send_next = jnp.swapaxes(edge(cols - 2, cols, 2), 1, 2)
@@ -248,8 +247,6 @@
     row_halo = jnp.concatenate(
         [below, jnp.zeros((total, 12, cols + PAD), jnp.float32), above], 1
     )
-    colf, colm = col_halo[: 2 * planes], col_halo[2 * planes :].astype(jnp.int32)
-    rowf, rowm = row_halo[: 2 * planes], row_halo[2 * planes :].astype(jnp.int32)
     high = rows + 2 * BASE
     width = cols + PAD
     f32 = jnp.float32
@@ -260,7 +257,7 @@
             jax.ShapeDtypeStruct((planes, rows, cols), f32),
             jax.ShapeDtypeStruct((gx, 2, rows, cols // parts), jnp.bfloat16),
         ),
-        in_specs=[ANY, ANY, ANY, VM, VM, VM, VM, SM, VM, VM],
+        in_specs=[ANY, ANY, ANY, VM, VM, SM, VM, VM],
         out_specs=(ANY, ANY, VM),
         scratch_shapes=[
             pltpu.VMEM((planes, high, width), f32),
@@ -274,7 +271,7 @@
         compiler_params=pltpu.CompilerParams(vmem_limit_bytes=BIG),
         name="yee",
     )(
-        e, h, material, colf, colm, rowf, rowm,
+        e, h, material, col_halo, row_halo,
         eps_table, jnp.swapaxes(src_pos, 0, 1), src_amp[None, :],
     )
     return out
@@ -317,39 +314,46 @@
     )(a_re, a_im, b_re, b_im)
 
 
-def rows_kernel(mix, tab, v, out):
-    nu = tab.shape[2]
+def rows_kernel(mix, tab, v, *outs):
+    group, _, nu, depth = tab.shape
     span = v.shape[3]
-    left = tab[0].reshape(2 * nu, tab.shape[3])
+    left = tab[...].reshape(group * 2 * nu, depth)
     got = []
     for which in range(2):
         right = v[:, which].reshape(-1, span)
         both = jnp.dot(left, right, preferred_element_type=jnp.float32)
-        got.append((both[:nu], both[nu:]))
-    (s_re, s_im), (d_re, d_im) = got
+        got.append(both.reshape(group, 2, nu, span))
     for f in range(NF):
         p_re, p_im, q_re, q_im = (mix[f, i] for i in range(4))
-        re = p_re * s_re - p_im * s_im + (q_re * d_re - q_im * d_im)
-        im = p_re * s_im + p_im * s_re + (q_re * d_im + q_im * d_re)
-        out[0, f, 0] = re.astype(jnp.bfloat16)
-        out[0, f, 1] = im.astype(jnp.bfloat16)
-
-
-def cols_kernel(g, tab, out):
-    parts, span = g.shape[1], g.shape[5]
-    width = tab.shape[2]
-    shares = out.shape[0]
-    vb = out.shape[4]
+        for b in range(group):
+            s_re, s_im = got[0][b, 0], got[0][b, 1]
+            d_re, d_im = got[1][b, 0], got[1][b, 1]
+            re = p_re * s_re - p_im * s_im + (q_re * d_re - q_im * d_im)
+            im = p_re * s_im + p_im * s_re + (q_re * d_im + q_im * d_re)
+            outs[f][b, 0] = re.astype(jnp.bfloat16)
+            outs[f][b, 1] = im.astype(jnp.bfloat16)
+
+
+def cols_kernel(g, tab, out, left):
+    parts, nu, span = g.shape[1], g.shape[3], g.shape[4]
+
+    @pl.when(pl.program_id(0) == 0)
+    def _():
+        for k in range(4):
+            for part in range(parts):
+                for c in range(2):
+                    left[c, k * nu : (k + 1) * nu, part * span : (part + 1) * span] = g[
+                        k, part, c
+                    ]
+
     y_re = tab[0, 0]
     y_im = tab[0, 1]
-    g_re = jnp.concatenate([g[0, p, 0, 0] for p in range(parts)], 1)
-    g_im = jnp.concatenate([g[0, p, 0, 1] for p in range(parts)], 1)
     dot = functools.partial(jnp.dot, preferred_element_type=jnp.float32)
-    re = dot(g_re, y_re) - dot(g_im, y_im)
-    im = dot(g_re, y_im) + dot(g_im, y_re)
-    for share in range(shares):
-        out[share, 0, 0] = re[:, share * vb : (share + 1) * vb].astype(out.dtype)
-        out[share, 0, 1] = im[:, share * vb : (share + 1) * vb].astype(out.dtype)
+    re = dot(left[0], y_re) - dot(left[1], y_im)
+    im = dot(left[0], y_im) + dot(left[1], y_re)
+    for k in range(4):
+        out[0, k, 0] = re[k * nu : (k + 1) * nu].astype(out.dtype)
+        out[0, k, 1] = im[k * nu : (k + 1) * nu].astype(out.dtype)
 
 
 def on_device(e_field, h_field, material, eps_table, src_pos, src_amp, freqs):
@@ -373,36 +377,44 @@
     mix = jnp.stack(
         [turn_re * half_re, turn_im * half_re, -turn_im * half_im, turn_re * half_im], 1
     )
-    g = pl.pallas_call(
+    group = 2
+    halves = pl.pallas_call(
         rows_kernel,
-        grid=(gx,),
-        out_shape=jax.ShapeDtypeStruct((gx, NF, 2, nu, span), bf16),
+        grid=(gx // group,),
+        out_shape=[jax.ShapeDtypeStruct((gx, 2, nu, span), bf16)] * NF,
         in_specs=[
             SM,
-            pl.BlockSpec((1, 2, nu, grid_rows), lambda i: (i, 0, 0, 0)),
+            pl.BlockSpec((group, 2, nu, grid_rows), lambda i: (i, 0, 0, 0)),
             pl.BlockSpec((gx, 2, rows, span), lambda i: (0, 0, 0, 0)),
         ],
-        out_specs=pl.BlockSpec((1, NF, 2, nu, span), lambda i: (i, 0, 0, 0, 0)),
+        out_specs=[pl.BlockSpec((group, 2, nu, span), lambda i: (i, 0, 0, 0))] * NF,
         compiler_params=pltpu.CompilerParams(vmem_limit_bytes=BIG),
         name="rows",
     )(mix, x_tab, got)
-    moved = lax.all_to_all(g, "gx", split_axis=0, concat_axis=0, tiled=True)
-    moved = moved.reshape(4, parts, NF, 2, nu, span)
-    share = pl.pallas_call(
-        cols_kernel,
-        grid=(NF, 4),
-        out_shape=jax.ShapeDtypeStruct((gy, NF * 4, 2, nu, vb), bf16),
-        in_specs=[
-            pl.BlockSpec((1, parts, 1, 2, nu, span), lambda f, k: (k, 0, f, 0, 0, 0)),
-            pl.BlockSpec((1, 2, cols, NA), lambda f, k: (0, 0, 0, 0)),
-        ],
-        out_specs=pl.BlockSpec((gy, 1, 2, nu, vb), lambda f, k: (0, f * 4 + k, 0, 0, 0)),
-        compiler_params=pltpu.CompilerParams(vmem_limit_bytes=BIG),
-        name="cols",
-    )(moved, y_tab)
     inv_norm = 1.0 / math.sqrt(grid_rows * grid_cols)
-    summed = lax.psum_scatter(share, "gy", scatter_dimension=0, tiled=True)
-    far = jnp.transpose(summed[0].astype(jnp.float32) * inv_norm, (2, 0, 1, 3))
+    fars = []
+    for g in halves:
+        moved = lax.all_to_all(g, "gx", split_axis=0, concat_axis=0, tiled=True)
+        moved = moved.reshape(4, parts, 2, nu, span)
+        share = pl.pallas_call(
+            cols_kernel,
+            grid=(gy,),
+            out_shape=jax.ShapeDtypeStruct((gy, 4, 2, nu, vb), bf16),
+            in_specs=[
+                pl.BlockSpec((4, parts, 2, nu, span), lambda j: (0, 0, 0, 0, 0)),
+                pl.BlockSpec((1, 2, cols, vb), lambda j: (0, 0, 0, j)),
+            ],
+            out_specs=pl.BlockSpec((1, 4, 2, nu, vb), lambda j: (j, 0, 0, 0, 0)),
+            scratch_shapes=[pltpu.VMEM((2, 4 * nu, cols), bf16)],
+            compiler_params=pltpu.CompilerParams(vmem_limit_bytes=BIG),
+            cost_estimate=pl.CostEstimate(
+                flops=64 * nu * cols * NA, bytes_accessed=16 * nu * NA, transcendentals=0
+            ),
+            name="cols",
+        )(moved, y_tab)
+        summed = lax.psum_scatter(share, "gy", scatter_dimension=0, tiled=True)
+        fars.append(jnp.transpose(summed[0].astype(jnp.float32) * inv_norm, (2, 0, 1, 3)))
+    far = jnp.concatenate(fars, 1)
     shape = e_field.shape
     return (e_new.reshape(shape), h_new.reshape(shape), far)
 

time: 236 us -> 231 us (0.979)
  waiting for transfers between devices: 104 us -> 79.2 us
  blocking collectives: 0 us -> 18.4 us
  other arithmetic: 16.4 us -> 19.2 us
  local copies, waits for them, and re-layouts: 24.1 us -> 21.5 us
    all_to_all x0 -> x1, blocking collectives: none -> 18.4 us  [on_device(): moved = lax.all_to_all(g, 'gx', split_axis=0, concat_axis=0, tiled=True)]
    reduce_scatter x1 -> x2, waiting for transfers between devices: 75.4 us -> 60.8 us  [on_device(): summed = lax.psum_scatter(share, 'gy', scatter_dimension=0, tiled=True)]
    all_to_all x1, waiting for transfers between devices: 18.8 us -> 7.59 us  [on_device(): moved = lax.all_to_all(g, 'gx', split_axis=0, concat_axis=0, tiled=True)]
    slice x2 -> x0, local copies, waits for them, and re-layouts: 2.53 us -> none  [the longest x1 1.6 us: yee(): col_halo[:2 * planes]]
    slice x11 -> x8, local copies, waits for them, and re-layouts: 10.8 us -> 9.2 us  [edge(): cut = lambda a: lax.slice_in_dim(a, low, high, axis=dim)]
    pallas_call x2 -> x3, Pallas kernels: 20.7 us -> 20.7 us  [the longest x2 11.4 us: on_device(): pl.pallas_call(cols_kernel, grid=(gy,), out_shape=jax.ShapeDtypeStruct((g...]
  transfers between devices with their start and end apart: 7 -> 8, of which waited for: 3 -> 5; matrix products, arithmetic and copies ran while one was open for 7% -> 8% of each run, Pallas kernels for 6% -> 8%
where the time goes in v2:
time: 231 us; the launch traced here: 230 us
  waiting for transfers between devices  79.2 us (34%)
  Pallas kernels  55.5 us (24%)
  starting transfers between devices  22 us (10%)
  local copies, waits for them, and re-layouts  21.5 us (9%)
  other arithmetic  19.2 us (8%)
  blocking collectives  18.4 us (8%)
  between operations  14.3 us (6%)
    reduce_scatter x2, waiting for transfers between devices, on_device(): summed = lax.psum_scatter(share, 'gy', scatter_dimension=0, tiled=True)  60.8 us
    pallas_call x1, Pallas kernels, yee(): pl.pallas_call(functools.partial(yee_kernel, grid_rows, grid_cols, parts)...  21.7 us
    all_to_all x1, blocking collectives, on_device(): moved = lax.all_to_all(g, 'gx', split_axis=0, concat_axis=0, tiled=True)  18.4 us
    pallas_call x2, Pallas kernels, table(): pl.pallas_call(table_kernel, grid=(blocks,), out_shape=jax.ShapeDtypeStru...  13.1 us
    pallas_call x2, Pallas kernels, on_device(): pl.pallas_call(cols_kernel, grid=(gy,), out_shape=jax.ShapeDtypeStruct((g...  11.4 us
    ppermute x4, starting transfers between devices, shifted(): return lax.ppermute(block, axis, route)  11.2 us
    all_to_all x1, waiting for transfers between devices, on_device(): got = lax.all_to_all(sd, 'gx', split_axis=0, concat_axis=0, tiled=True)  9.88 us
    neg x4, other arithmetic, unit(): return (jnp.cos(angle), -jnp.sin(angle))  9.68 us
  transfers between devices with their start and end apart: 8, of which 5 were waited for; matrix products, arithmetic and copies ran while one was open for 8% of the time, Pallas kernels for 8%

profile of v2, /device:TPU:0, one launch (start us, length us, event | category | flops | bytes accessed | tf_op | source)
XLA Modules:
  0.0 230.0 jit_solution(1556646393603733731)
XLA Ops:
  7.2 2.0 fusion.20
  10.2 2.0 fusion.21
  17.6 5.6 %collective-permute-start.1 = (f32[21,2,256]{2,1,0:T(2,128)S(1)}, f32[21,2,256]{2,1,0:T(2,128)S(1)}, u32[]{:S(2)}, u32[]{:S(2)}) collective-permute-start(f32[21,2,256]{2,1,0:T(2,128)S(1)} %maximum_bitcast_fusion.1), channel_id=1, source_target_pairs={{0,1},{1,2},{2,3},{4,5},{5,6},{6,7},{8,9},{9,10},{10,11},{12,13},{... | collective-permute-start | bytes 129032 | tf_op jit(solution)/shard_map/ppermute | solution.py:34
  25.3 2.4 %copy.31 = f32[21,2,256]{1,2,0:T(8,128)} copy(f32[21,2,256]{2,1,0:T(2,128)S(1)} %collective-permute-done) | data formatting | bytes 86016 | tf_op jit(solution)/shard_map/ppermute | solution.py:34
  27.7 2.4 %copy.35 = f32[21,2,256]{1,2,0:T(8,128)} copy(f32[21,2,256]{2,1,0:T(2,128)S(1)} %collective-permute-done.1) | data formatting | bytes 86016 | tf_op jit(solution)/shard_map/ppermute | solution.py:34
  30.1 3.4 %pad_maximum_fusion.colh = f32[21,256,128]{2,1,0:T(8,128)S(1)} fusion(f32[21,256,2]{2,1,0:T(8,128)} %bitcast.31, f32[21,256,2]{2,1,0:T(8,128)} %bitcast.30, f32[128]{0:T(128)S(1)} %pad.18.clone), kind=kLoop, calls=%fused_computation | loop fusion | flops 1376256 | bytes 2839040 | tf_op jit(solution)/shard_map/concatenate | solution.py:240
  34.9 3.0 %collective-permute-start.3 = (f32[21,2,640]{2,1,0:T(2,128)S(1)}, f32[21,2,640]{2,1,0:T(2,128)S(1)}, u32[]{:S(2)}, u32[]{:S(2)}) collective-permute-start(f32[21,2,640]{2,1,0:T(2,128)S(1)} %pad_maximum_fusion.4), channel_id=1, source_target_pairs={{0,4},{4,8},{8,12},{12,16},{16,20},{20,24},{24,28},{1,5},{5,9},{9,... | collective-permute-start | bytes 322568 | tf_op jit(solution)/shard_map/ppermute | solution.py:34
  39.9 21.7 %yee.1 = (f32[9,256,512]{2,1,0:T(8,128)}, f32[9,256,512]{2,1,0:T(8,128)}, bf16[8,2,256,256]{3,2,1,0:T(8,128)(2,1)}) custom-call(f32[9,256,512]{2,1,0:T(8,128)} %bitcast.34, f32[9,256,512]{2,1,0:T(8,128)} %bitcast.37, s32[3,256,512]{2,1,0:T(8,128)} %m_hbm.1, f32[21,256,128]{2,1,0:T(8,128)} %copy-done, f32[21,16,640]{2,1,0:T(8,128)} %pad_maximum_fusion.2.rowh, ...), custom_call_target="tpu_custom_call" | custom-call | tf_op jit(solution)/shard_map/yee/pallas_call | solution.py:253
  61.7 7.1 %all-to-all-start = ((bf16[8,2,256,256]{3,2,1,0:T(8,128)(2,1)}), bf16[8,2,256,256]{3,2,1,0:T(8,128)(2,1)S(1)}, u32[]{:S(2)}, u32[]{:S(2)}) async-start(bf16[8,2,256,256]{3,2,1,0:T(8,128)(2,1)} %get-tuple-element.10), calls=%async_computation | async-start | bytes 4194304 | tf_op jit(solution)/shard_map/all_to_all | solution.py:374
  69.6 3.3 %sine_negate_fusion = (f32[1024,128]{1,0:T(8,128)}, f32[1024,128]{1,0:T(8,128)}) fusion(s32[1024]{0:T(1024)S(1)} %iota_add_fusion), kind=kLoop, calls=%fused_computation.11 | loop fusion | flops 1966080 | bytes 1052672 | tf_op jit(solution)/shard_map/neg | solution.py:292
  72.8 2.8 %sine_negate_fusion.1 = (f32[1024,16]{1,0:T(8,128)}, f32[1024,16]{1,0:T(8,128)}) fusion(f32[1024,16]{1,0:T(8,128)S(1)} %copy.40), kind=kLoop, calls=%fused_computation.14 | loop fusion | flops 32768 | bytes 196608 | tf_op jit(solution)/shard_map/neg | solution.py:292
  75.6 9.3 %chirp.2.tab = bf16[8,2,128,2048]{3,2,1,0:T(8,128)(2,1)} custom-call(f32[1024,16]{1,0:T(8,128)} %get-tuple-element.37.a_re, f32[1024,16]{1,0:T(8,128)} %get-tuple-element.36.a_im, f32[1024,128]{1,0:T(8,128)} %get-tuple-element.41.b_re, f32[1024,128]{1,0:T(8,128)} %get-tuple-element.40.b_im), custom_call_target="tpu_custom_call" | custom-call | flops 16777216 | bytes 8388608 | tf_op jit(solution)/shard_map/chirp/pallas_call | solution.py:304
  85.5 9.9 %all-to-all-done.v = bf16[8,2,256,256]{3,2,1,0:T(8,128)(2,1)S(1)} async-done(((bf16[8,2,256,256]{3,2,1,0:T(8,128)(2,1)}), bf16[8,2,256,256]{3,2,1,0:T(8,128)(2,1)S(1)}, u32[]{:S(2)}, u32[]{:S(2)}) %all-to-all-start) | async-done | bytes 2097184 | tf_op jit(solution)/shard_map/all_to_all | solution.py:374
  96.7 9.3 %rows.1 = (bf16[8,2,128,256]{3,2,1,0:T(8,128)(2,1)}, bf16[8,2,128,256]{3,2,1,0:T(8,128)(2,1)}) custom-call(f32[2,4]{1,0:T(2,128)} %pad_maximum_fusion.5.mix, bf16[8,2,128,2048]{3,2,1,0:T(8,128)(2,1)} %chirp.2.tab, bf16[8,2,256,256]{3,2,1,0:T(8,128)(2,1)} %copy-done.1), custom_call_target="tpu_custom_call" | custom-call | tf_op jit(solution)/shard_map/rows/pallas_call | solution.py:381
  106.0 3.6 %all-to-all-start.1 = ((bf16[8,2,128,256]{3,2,1,0:T(8,128)(2,1)}), bf16[8,2,128,256]{3,2,1,0:T(8,128)(2,1)S(1)}, u32[]{:S(2)}, u32[]{:S(2)}) async-start(bf16[8,2,128,256]{3,2,1,0:T(8,128)(2,1)} %get-tuple-element.11), calls=%async_computation.1 | async-start | bytes 2097152 | tf_op jit(solution)/shard_map/all_to_all | solution.py:397
  109.9 2.0 sine_negate_fusion.2
  113.5 3.8 %chirp.3.tab = bf16[1,2,512,1024]{3,2,1,0:T(8,128)(2,1)} custom-call(f32[512,8]{1,0:T(8,128)} %get-tuple-element.39.a_re, f32[512,8]{1,0:T(8,128)} %get-tuple-element.38.a_im, f32[512,128]{1,0:T(8,128)} %get-tuple-element.43.b_re, f32[512,128]{1,0:T(8,128)} %get-tuple-element.42.b_im), custom_call_target="tpu_custom_call" | custom-call | flops 4194304 | bytes 2097152 | tf_op jit(solution)/shard_map/chirp/pallas_call | solution.py:304
  117.3 7.6 %all-to-all-done.1 = bf16[8,2,128,256]{3,2,1,0:T(8,128)(2,1)S(1)} async-done(((bf16[8,2,128,256]{3,2,1,0:T(8,128)(2,1)}), bf16[8,2,128,256]{3,2,1,0:T(8,128)(2,1)S(1)}, u32[]{:S(2)}, u32[]{:S(2)}) %all-to-all-start.1) | async-done | bytes 1048608 | tf_op jit(solution)/shard_map/all_to_all | solution.py:397
  125.9 5.7 %cols.2 = bf16[4,4,2,128,256]{4,3,2,1,0:T(8,128)(2,1)} custom-call(bf16[4,2,2,128,256]{4,3,2,1,0:T(8,128)(2,1)} %bitcast.38, bf16[1,2,512,1024]{3,2,1,0:T(8,128)(2,1)} %chirp.3.tab), custom_call_target="tpu_custom_call" | custom-call | flops 4294967296 | bytes 2097152 | tf_op jit(solution)/shard_map/cols/pallas_call | solution.py:399
  132.8 18.4 %all_to_all.15 = bf16[8,2,128,256]{3,2,1,0:T(8,128)(2,1)} all-to-all(bf16[8,2,128,256]{3,2,1,0:T(8,128)(2,1)S(1)} %copy-done.2), channel_id=1, replica_groups=mesh['gx'=8,'gy'=4] {'gx'}, dimensions={0} | all-to-all | bytes 2097152 | tf_op jit(solution)/shard_map/all_to_all | solution.py:397
  151.3 5.7 %cols.3 = bf16[4,4,2,128,256]{4,3,2,1,0:T(8,128)(2,1)} custom-call(bf16[4,2,2,128,256]{4,3,2,1,0:T(8,128)(2,1)} %bitcast.39, bf16[1,2,512,1024]{3,2,1,0:T(8,128)(2,1)} %chirp.3.tab), custom_call_target="tpu_custom_call" | custom-call | flops 4294967296 | bytes 2097152 | tf_op jit(solution)/shard_map/cols/pallas_call | solution.py:399
  157.0 16.8 %reduce-scatter.3.cloned.1.call-done = bf16[1,4,2,128,256]{4,3,2,1,0:T(8,128)(2,1)} async-done(((bf16[4,4,2,128,256]{4,3,2,1,0:T(8,128)(2,1)}), bf16[1,4,2,128,256]{4,3,2,1,0:T(8,128)(2,1)}) %reduce-scatter.3.cloned.1.call-update) | async-done | bytes 524304 | tf_op jit(solution)/shard_map/reduce_scatter | solution.py:415
  174.9 44.0 %reduce-scatter.5.cloned.1.call-done = bf16[1,4,2,128,256]{4,3,2,1,0:T(8,128)(2,1)} async-done(((bf16[4,4,2,128,256]{4,3,2,1,0:T(8,128)(2,1)}), bf16[1,4,2,128,256]{4,3,2,1,0:T(8,128)(2,1)}) %reduce-scatter.5.cloned.1.call-update) | async-done | bytes 524304 | tf_op jit(solution)/shard_map/reduce_scatter | solution.py:415
  220.3 2.9 %copy.42 = f32[128,8,2,256]{3,2,1,0:T(2,128)} copy(f32[128,8,2,256]{3,0,2,1:T(8,128)S(1)} %pad_maximum_fusion.1) | data formatting | bytes 4194304
  (59 shorter events, 21.1 us)
Async XLA Ops:
  15.4 10.0 %collective-permute-start = (f32[21,2,256]{2,1,0:T(2,128)S(1)}, f32[21,2,256]{2,1,0:T(2,128)S(1)}, u32[]{:S(2)}, u32[]{:S(2)}) collective-permute-start(f32[21,2,256]{2,1,0:T(2,128)S(1)} %maximum_bitcast_fusion), channel_id=1, source_target_pairs={{1,0},{2,1},{3,2},{5,4},{6,5},{7,6},{9,8},{10,9},{11,10},{13,12},{... | collective-permute-start | bytes 129032 | tf_op jit(solution)/shard_map/ppermute | solution.py:34
  17.6 10.1 %collective-permute-start.1 = (f32[21,2,256]{2,1,0:T(2,128)S(1)}, f32[21,2,256]{2,1,0:T(2,128)S(1)}, u32[]{:S(2)}, u32[]{:S(2)}) collective-permute-start(f32[21,2,256]{2,1,0:T(2,128)S(1)} %maximum_bitcast_fusion.1), channel_id=1, source_target_pairs={{0,1},{1,2},{2,3},{4,5},{5,6},{6,7},{8,9},{9,10},{10,11},{12,13},{... | collective-permute-start | bytes 129032 | tf_op jit(solution)/shard_map/ppermute | solution.py:34
  33.5 6.5 %copy-start = (f32[21,256,128]{2,1,0:T(8,128)}, f32[21,256,128]{2,1,0:T(8,128)S(1)}, u32[]{:S(2)}) copy-start(f32[21,256,128]{2,1,0:T(8,128)S(1)} %pad_maximum_fusion.colh) | copy-start | bytes 8257540
  33.6 4.5 %collective-permute-start.2 = (f32[21,2,640]{2,1,0:T(2,128)S(1)}, f32[21,2,640]{2,1,0:T(2,128)S(1)}, u32[]{:S(2)}, u32[]{:S(2)}) collective-permute-start(f32[21,2,640]{2,1,0:T(2,128)S(1)} %pad_maximum_fusion.3), channel_id=1, source_target_pairs={{4,0},{8,4},{12,8},{16,12},{20,16},{24,20},{28,24},{5,1},{9,5},{13... | collective-permute-start | bytes 322568 | tf_op jit(solution)/shard_map/ppermute | solution.py:34
  34.9 4.0 %collective-permute-start.3 = (f32[21,2,640]{2,1,0:T(2,128)S(1)}, f32[21,2,640]{2,1,0:T(2,128)S(1)}, u32[]{:S(2)}, u32[]{:S(2)}) collective-permute-start(f32[21,2,640]{2,1,0:T(2,128)S(1)} %pad_maximum_fusion.4), channel_id=1, source_target_pairs={{0,4},{4,8},{8,12},{12,16},{16,20},{20,24},{24,28},{1,5},{5,9},{9,... | collective-permute-start | bytes 322568 | tf_op jit(solution)/shard_map/ppermute | solution.py:34
  61.7 7.1 %copy-start.4 = (f32[2]{0:T(128)S(1)}, f32[2]{0:T(128)}, u32[]{:S(2)}) copy-start(f32[2]{0:T(128)} %param.13) | copy-start | bytes 28
  61.7 33.7 %all-to-all-start = ((bf16[8,2,256,256]{3,2,1,0:T(8,128)(2,1)}), bf16[8,2,256,256]{3,2,1,0:T(8,128)(2,1)S(1)}, u32[]{:S(2)}, u32[]{:S(2)}) async-start(bf16[8,2,256,256]{3,2,1,0:T(8,128)(2,1)} %get-tuple-element.10), calls=%async_computation | async-start | bytes 4194304 | tf_op jit(solution)/shard_map/all_to_all | solution.py:374
  95.4 1.3 copy-start.1
  106.0 18.9 %all-to-all-start.1 = ((bf16[8,2,128,256]{3,2,1,0:T(8,128)(2,1)}), bf16[8,2,128,256]{3,2,1,0:T(8,128)(2,1)S(1)}, u32[]{:S(2)}, u32[]{:S(2)}) async-start(bf16[8,2,128,256]{3,2,1,0:T(8,128)(2,1)} %get-tuple-element.11), calls=%async_computation.1 | async-start | bytes 2097152 | tf_op jit(solution)/shard_map/all_to_all | solution.py:397
  109.6 64.2 %reduce-scatter.3.cloned.1.call-start = ((), (), s32[]{:S(2)}) async-start(), calls=%async_computation.5 | async-start | bytes 2621440 | tf_op jit(solution)/shard_map/reduce_scatter | solution.py:415
  124.9 1.0 copy-start.3
  131.6 1.2 copy-start.2
  131.6 87.3 %reduce-scatter.5.cloned.1.call-start = ((), (), s32[]{:S(2)}) async-start(), calls=%async_computation.6 | async-start | bytes 2621440 | tf_op jit(solution)/shard_map/reduce_scatter | solution.py:415
Sparse Core Ops, SparseCore 0:
  131.7 41.9 reduce-scatter.2
  176.1 42.8 reduce-scatter.4

commit v3 on v2

--- a/solution.py
+++ b/solution.py
@@ -21,6 +21,8 @@
 
 BASE = 32
 CHUNK = 16
+SETS = 2
+EACH = 4 // SETS
 PAD = 128
 ANY = pl.BlockSpec(memory_space=pl.ANY)
 VM = pl.BlockSpec(memory_space=pltpu.VMEM)
@@ -35,11 +37,11 @@
 
 
 def yee_kernel(
-    grid_rows, grid_cols, parts,
+    grid_rows, grid_cols, gx,
     e_hbm, h_hbm, m_hbm, colh, rowh, eps, pos, amp,
-    e_out, h_out, sd_out,
-    e_ext, h_ext, m_main, scale, src, first, sems,
+    e_out, h_out, *rest,
 ):
+    sd_outs, (e_ext, h_ext, m_main, scale, src, first, sems) = rest[:SETS], rest[SETS:]
     rows, cols = m_main.shape[1:]
     width = cols + PAD
     high = e_ext.shape[1]
@@ -190,13 +192,13 @@
                     if last:
                         old = first[item, now, :]
                         here = pl.ds(r - BASE, CHUNK)
-                        span = cols // parts
+                        span = cols // gx
+                        place = (item % EACH) * span
                         for which, value in enumerate((old + face, face - old)):
-                            value = value.astype(jnp.bfloat16)
-                            for part in range(parts):
-                                sd_out[item * parts + part, which, here, :] = value[
-                                    :, part * span : (part + 1) * span
-                                ]
+                            lo = which * EACH * span + place
+                            for j in range(gx):
+                                piece = value[:, j * span : (j + 1) * span].astype(jnp.bfloat16)
+                                sd_outs[item // EACH][j, here, lo : lo + span] = piece
                     else:
                         first[item, now, :] = face
         return carry
@@ -219,7 +221,6 @@
 def yee(e_field, h_field, material, eps_table, src_pos, src_amp):
     rows, cols = material.shape[1:]
     gx = lax.axis_size("gx")
-    parts = gx // 4
     grid_rows = rows * gx
     grid_cols = cols * lax.axis_size("gy")
     planes = 3 * LZ
@@ -251,14 +252,14 @@
     width = cols + PAD
     f32 = jnp.float32
     out = pl.pallas_call(
-        functools.partial(yee_kernel, grid_rows, grid_cols, parts),
+        functools.partial(yee_kernel, grid_rows, grid_cols, gx),
         out_shape=(
             jax.ShapeDtypeStruct((planes, rows, cols), f32),
             jax.ShapeDtypeStruct((planes, rows, cols), f32),
-            jax.ShapeDtypeStruct((gx, 2, rows, cols // parts), jnp.bfloat16),
-        ),
+        )
+        + (jax.ShapeDtypeStruct((gx, rows, 2 * EACH * (cols // gx)), jnp.bfloat16),) * SETS,
         in_specs=[ANY, ANY, ANY, VM, VM, SM, VM, VM],
-        out_specs=(ANY, ANY, VM),
+        out_specs=(ANY, ANY) + (VM,) * SETS,
         scratch_shapes=[
             pltpu.VMEM((planes, high, width), f32),
             pltpu.VMEM((planes, high, width), f32),
@@ -314,54 +315,53 @@
     )(a_re, a_im, b_re, b_im)
 
 
-def rows_kernel(mix, tab, v, *outs):
+def rows_kernel(mix, tab, v, out):
     group, _, nu, depth = tab.shape
-    span = v.shape[3]
+    half = v.shape[2] // 2
     left = tab[...].reshape(group * 2 * nu, depth)
-    got = []
-    for which in range(2):
-        right = v[:, which].reshape(-1, span)
-        both = jnp.dot(left, right, preferred_element_type=jnp.float32)
-        got.append(both.reshape(group, 2, nu, span))
-    for f in range(NF):
-        p_re, p_im, q_re, q_im = (mix[f, i] for i in range(4))
-        for b in range(group):
-            s_re, s_im = got[0][b, 0], got[0][b, 1]
-            d_re, d_im = got[1][b, 0], got[1][b, 1]
+    right = v[...].reshape(depth, 2 * half)
+    both = jnp.dot(left, right, preferred_element_type=jnp.float32)
+    both = both.reshape(group, 2, nu, 2 * half)
+    for b in range(group):
+        s_re, s_im = both[b, 0, :, :half], both[b, 1, :, :half]
+        d_re, d_im = both[b, 0, :, half:], both[b, 1, :, half:]
+        for f in range(NF):
+            p_re, p_im, q_re, q_im = (mix[f, i] for i in range(4))
             re = p_re * s_re - p_im * s_im + (q_re * d_re - q_im * d_im)
             im = p_re * s_im + p_im * s_re + (q_re * d_im + q_im * d_re)
-            outs[f][b, 0] = re.astype(jnp.bfloat16)
-            outs[f][b, 1] = im.astype(jnp.bfloat16)
+            out[b, f, 0] = re.astype(jnp.bfloat16)
+            out[b, f, 1] = im.astype(jnp.bfloat16)
 
 
 def cols_kernel(g, tab, out, left):
-    parts, nu, span = g.shape[1], g.shape[3], g.shape[4]
+    gx, _, _, nu, wide = g.shape
+    span = wide // EACH
 
     @pl.when(pl.program_id(0) == 0)
     def _():
-        for k in range(4):
-            for part in range(parts):
-                for c in range(2):
-                    left[c, k * nu : (k + 1) * nu, part * span : (part + 1) * span] = g[
-                        k, part, c
-                    ]
+        for f in range(NF):
+            for c in range(2):
+                got = [g[j, f, c].astype(jnp.float32) for j in range(gx)]
+                for k in range(EACH):
+                    at = (f * EACH + k) * nu
+                    row = [piece[:, k * span : (k + 1) * span] for piece in got]
+                    left[c, at : at + nu, :] = jnp.concatenate(row, 1).astype(jnp.bfloat16)
 
     y_re = tab[0, 0]
     y_im = tab[0, 1]
     dot = functools.partial(jnp.dot, preferred_element_type=jnp.float32)
     re = dot(left[0], y_re) - dot(left[1], y_im)
     im = dot(left[0], y_im) + dot(left[1], y_re)
-    for k in range(4):
-        out[0, k, 0] = re[k * nu : (k + 1) * nu].astype(out.dtype)
-        out[0, k, 1] = im[k * nu : (k + 1) * nu].astype(out.dtype)
+    for i in range(NF * EACH):
+        out[0, i, 0] = re[i * nu : (i + 1) * nu].astype(out.dtype)
+        out[0, i, 1] = im[i * nu : (i + 1) * nu].astype(out.dtype)
 
 
 def on_device(e_field, h_field, material, eps_table, src_pos, src_amp, freqs):
     rows, cols = material.shape[1:]
     gx, gy = lax.axis_size("gx"), lax.axis_size("gy")
     grid_rows, grid_cols = rows * gx, cols * gy
-    parts = gx // 4
-    span = cols // parts
+    wide = EACH * (cols // gx)
     nu = NA // gx
     vb = NA // gy
     col_start = lax.axis_index("gy") * cols
@@ -370,51 +370,51 @@
     x_tab = table(angle_index - NA // 2, 0, grid_rows, zoom_factor * grid_rows, gx)
     y_cells = col_start + jnp.arange(cols, dtype=jnp.int32)
     y_tab = table(y_cells, NA // 4, NA, zoom_factor * grid_cols, 1)
-    e_new, h_new, sd = yee(e_field, h_field, material, eps_table, src_pos, src_amp)
-    got = lax.all_to_all(sd, "gx", split_axis=0, concat_axis=0, tiled=True)
+    e_new, h_new, *sd = yee(e_field, h_field, material, eps_table, src_pos, src_amp)
     turn_re, turn_im = jnp.cos(1.5 * freqs), jnp.sin(1.5 * freqs)
     half_re, half_im = jnp.cos(0.5 * freqs), jnp.sin(0.5 * freqs)
     mix = jnp.stack(
         [turn_re * half_re, turn_im * half_re, -turn_im * half_im, turn_re * half_im], 1
     )
     group = 2
-    halves = pl.pallas_call(
-        rows_kernel,
-        grid=(gx // group,),
-        out_shape=[jax.ShapeDtypeStruct((gx, 2, nu, span), bf16)] * NF,
-        in_specs=[
-            SM,
-            pl.BlockSpec((group, 2, nu, grid_rows), lambda i: (i, 0, 0, 0)),
-            pl.BlockSpec((gx, 2, rows, span), lambda i: (0, 0, 0, 0)),
-        ],
-        out_specs=[pl.BlockSpec((group, 2, nu, span), lambda i: (i, 0, 0, 0))] * NF,
-        compiler_params=pltpu.CompilerParams(vmem_limit_bytes=BIG),
-        name="rows",
-    )(mix, x_tab, got)
     inv_norm = 1.0 / math.sqrt(grid_rows * grid_cols)
     fars = []
-    for g in halves:
+    for sent in sd:
+        got = lax.all_to_all(sent, "gx", split_axis=0, concat_axis=0, tiled=True)
+        g = pl.pallas_call(
+            rows_kernel,
+            grid=(gx // group,),
+            out_shape=jax.ShapeDtypeStruct((gx, NF, 2, nu, wide), bf16),
+            in_specs=[
+                SM,
+                pl.BlockSpec((group, 2, nu, grid_rows), lambda i: (i, 0, 0, 0)),
+                pl.BlockSpec((gx, rows, 2 * wide), lambda i: (0, 0, 0)),
+            ],
+            out_specs=pl.BlockSpec((group, NF, 2, nu, wide), lambda i: (i, 0, 0, 0, 0)),
+            compiler_params=pltpu.CompilerParams(vmem_limit_bytes=BIG),
+            name="rows",
+        )(mix, x_tab, got)
         moved = lax.all_to_all(g, "gx", split_axis=0, concat_axis=0, tiled=True)
-        moved = moved.reshape(4, parts, 2, nu, span)
         share = pl.pallas_call(
             cols_kernel,
             grid=(gy,),
-            out_shape=jax.ShapeDtypeStruct((gy, 4, 2, nu, vb), bf16),
+            out_shape=jax.ShapeDtypeStruct((gy, NF * EACH, 2, nu, vb), bf16),
             in_specs=[
-                pl.BlockSpec((4, parts, 2, nu, span), lambda j: (0, 0, 0, 0, 0)),
+                pl.BlockSpec((gx, NF, 2, nu, wide), lambda j: (0, 0, 0, 0, 0)),
                 pl.BlockSpec((1, 2, cols, vb), lambda j: (0, 0, 0, j)),
             ],
-            out_specs=pl.BlockSpec((1, 4, 2, nu, vb), lambda j: (j, 0, 0, 0, 0)),
-            scratch_shapes=[pltpu.VMEM((2, 4 * nu, cols), bf16)],
+            out_specs=pl.BlockSpec((1, NF * EACH, 2, nu, vb), lambda j: (j, 0, 0, 0, 0)),
+            scratch_shapes=[pltpu.VMEM((2, NF * EACH * nu, cols), bf16)],
             compiler_params=pltpu.CompilerParams(vmem_limit_bytes=BIG),
             cost_estimate=pl.CostEstimate(
-                flops=64 * nu * cols * NA, bytes_accessed=16 * nu * NA, transcendentals=0
+                flops=16 * NF * EACH * nu * cols * NA, bytes_accessed=16 * nu * NA, transcendentals=0
             ),
             name="cols",
         )(moved, y_tab)
         summed = lax.psum_scatter(share, "gy", scatter_dimension=0, tiled=True)
-        fars.append(jnp.transpose(summed[0].astype(jnp.float32) * inv_norm, (2, 0, 1, 3)))
-    far = jnp.concatenate(fars, 1)
+        scaled = summed[0].astype(jnp.float32) * inv_norm
+        fars.append(jnp.transpose(scaled, (2, 0, 1, 3)).reshape(nu, NF, EACH, 2, vb))
+    far = jnp.concatenate(fars, 2).reshape(nu, NF * 4, 2, vb)
     shape = e_field.shape
     return (e_new.reshape(shape), h_new.reshape(shape), far)
 

time: 231 us -> 228 us (0.987)
  waiting for transfers between devices: 79.2 us -> 49.6 us
  blocking collectives: 18.4 us -> 38 us
  Pallas kernels: 55.5 us -> 61.4 us
    reduce_scatter x2, waiting for transfers between devices: 60.8 us -> 41 us  [on_device(): summed = lax.psum_scatter(share, 'gy', scatter_dimension=0, tiled=True)]
    all_to_all x0 -> x1, blocking collectives: none -> 18.4 us  [on_device(): got = lax.all_to_all(sent, 'gx', split_axis=0, concat_axis=0, tiled=True)]
    all_to_all x1, waiting for transfers between devices: 9.88 us -> 0.01 us  [on_device(): got = lax.all_to_all(sent, 'gx', split_axis=0, concat_axis=0, tiled=True)]
    pallas_call x2 -> x3, Pallas kernels: 31 us -> 36.2 us  [the longest x1 22.8 us: yee(): pl.pallas_call(functools.partial(yee_kernel, grid_rows, grid_cols, gx), o...]
    unnamed x13 -> x12, local copies, waits for them, and re-layouts: 6.71 us -> 3.44 us
    concatenate x0 -> x1, local copies, waits for them, and re-layouts: none -> 2.94 us  [on_device(): far = jnp.concatenate(fars, 2).reshape(nu, NF * 4, 2, vb)]
  transfers between devices with their start and end apart: 8 -> 8, of which waited for: 5 -> 3; matrix products, arithmetic and copies ran while one was open for 8% -> 8% of each run, Pallas kernels for 8% -> 11%
where the time goes in v3:
time: 228 us; the launch traced here: 226 us
  Pallas kernels  61.4 us (27%)
  waiting for transfers between devices  49.6 us (22%)
  blocking collectives  38 us (17%)
  starting transfers between devices  22.6 us (10%)
  local copies, waits for them, and re-layouts  21.2 us (9%)
  other arithmetic  19.1 us (8%)
  between operations  14.3 us (6%)
    reduce_scatter x2, waiting for transfers between devices, on_device(): summed = lax.psum_scatter(share, 'gy', scatter_dimension=0, tiled=True)  41 us
    pallas_call x1, Pallas kernels, yee(): pl.pallas_call(functools.partial(yee_kernel, grid_rows, grid_cols, gx), o...  22.8 us
    all_to_all x1, blocking collectives, on_device(): moved = lax.all_to_all(g, 'gx', split_axis=0, concat_axis=0, tiled=True)  19.6 us
    all_to_all x1, blocking collectives, on_device(): got = lax.all_to_all(sent, 'gx', split_axis=0, concat_axis=0, tiled=True)  18.4 us
    pallas_call x2, Pallas kernels, on_device(): pl.pallas_call(rows_kernel, grid=(gx // group,), out_shape=jax.ShapeDtype...  13.5 us
    pallas_call x2, Pallas kernels, table(): pl.pallas_call(table_kernel, grid=(blocks,), out_shape=jax.ShapeDtypeStru...  13.1 us
    pallas_call x2, Pallas kernels, on_device(): pl.pallas_call(cols_kernel, grid=(gy,), out_shape=jax.ShapeDtypeStruct((g...  12.1 us
    ppermute x4, starting transfers between devices, shifted(): return lax.ppermute(block, axis, route)  11.2 us
  transfers between devices with their start and end apart: 8, of which 3 were waited for; matrix products, arithmetic and copies ran while one was open for 8% of the time, Pallas kernels for 11%

profile of v3, /device:TPU:0, one launch (start us, length us, event | category | flops | bytes accessed | tf_op | source)
XLA Modules:
  0.0 226.2 jit_solution(1260062276713016705)
XLA Ops:
  7.2 2.0 fusion.20
  10.2 2.0 fusion.21
  17.6 5.6 %collective-permute-start.1 = (f32[21,2,256]{2,1,0:T(2,128)S(1)}, f32[21,2,256]{2,1,0:T(2,128)S(1)}, u32[]{:S(2)}, u32[]{:S(2)}) collective-permute-start(f32[21,2,256]{2,1,0:T(2,128)S(1)} %maximum_bitcast_fusion.1), channel_id=1, source_target_pairs={{0,1},{1,2},{2,3},{4,5},{5,6},{6,7},{8,9},{9,10},{10,11},{12,13},{... | collective-permute-start | bytes 129032 | tf_op jit(solution)/shard_map/ppermute | solution.py:36
  25.9 2.4 %copy.31 = f32[21,2,256]{1,2,0:T(8,128)} copy(f32[21,2,256]{2,1,0:T(2,128)S(1)} %collective-permute-done) | data formatting | bytes 86016 | tf_op jit(solution)/shard_map/ppermute | solution.py:36
  28.2 2.4 %copy.35 = f32[21,2,256]{1,2,0:T(8,128)} copy(f32[21,2,256]{2,1,0:T(2,128)S(1)} %collective-permute-done.1) | data formatting | bytes 86016 | tf_op jit(solution)/shard_map/ppermute | solution.py:36
  30.6 3.4 %pad_maximum_fusion.colh = f32[21,256,128]{2,1,0:T(8,128)S(1)} fusion(f32[21,256,2]{2,1,0:T(8,128)} %bitcast.32, f32[21,256,2]{2,1,0:T(8,128)} %bitcast.31, f32[128]{0:T(128)S(1)} %pad.18.clone), kind=kLoop, calls=%fused_computation | loop fusion | flops 1376256 | bytes 2839040 | tf_op jit(solution)/shard_map/concatenate | solution.py:241
  35.5 3.0 %collective-permute-start.3 = (f32[21,2,640]{2,1,0:T(2,128)S(1)}, f32[21,2,640]{2,1,0:T(2,128)S(1)}, u32[]{:S(2)}, u32[]{:S(2)}) collective-permute-start(f32[21,2,640]{2,1,0:T(2,128)S(1)} %pad_maximum_fusion.4), channel_id=1, source_target_pairs={{0,4},{4,8},{8,12},{12,16},{16,20},{20,24},{24,28},{1,5},{5,9},{9,... | collective-permute-start | bytes 322568 | tf_op jit(solution)/shard_map/ppermute | solution.py:36
  40.5 22.8 %yee.1 = (f32[9,256,512]{2,1,0:T(8,128)}, f32[9,256,512]{2,1,0:T(8,128)}, bf16[8,256,256]{2,1,0:T(8,128)(2,1)}, bf16[8,256,256]{2,1,0:T(8,128)(2,1)}) custom-call(f32[9,256,512]{2,1,0:T(8,128)} %bitcast.35, f32[9,256,512]{2,1,0:T(8,128)} %bitcast.38, s32[3,256,512]{2,1,0:T(8,128)} %m_hbm.1, f32[21,256,128]{2,1,0:T(8,128)} %copy-done, ...), custom_call_target="tpu_custom_call" | custom-call | tf_op jit(solution)/shard_map/yee/pallas_call | solution.py:254
  63.2 7.1 %all-to-all-start = ((bf16[8,256,256]{2,1,0:T(8,128)(2,1)}), bf16[8,256,256]{2,1,0:T(8,128)(2,1)S(1)}, u32[]{:S(2)}, u32[]{:S(2)}) async-start(bf16[8,256,256]{2,1,0:T(8,128)(2,1)} %get-tuple-element.9), calls=%async_computation | async-start | bytes 2097152 | tf_op jit(solution)/shard_map/all_to_all | solution.py:383
  70.7 3.3 %sine_negate_fusion = (f32[1024,128]{1,0:T(8,128)}, f32[1024,128]{1,0:T(8,128)}) fusion(s32[1024]{0:T(1024)S(1)} %iota_add_fusion), kind=kLoop, calls=%fused_computation.11 | loop fusion | flops 1966080 | bytes 1052672 | tf_op jit(solution)/shard_map/neg | solution.py:293
  73.9 2.8 %sine_negate_fusion.1 = (f32[1024,16]{1,0:T(8,128)}, f32[1024,16]{1,0:T(8,128)}) fusion(f32[1024,16]{1,0:T(8,128)S(1)} %copy.40), kind=kLoop, calls=%fused_computation.14 | loop fusion | flops 32768 | bytes 196608 | tf_op jit(solution)/shard_map/neg | solution.py:293
  76.7 9.3 %chirp.2.tab = bf16[8,2,128,2048]{3,2,1,0:T(8,128)(2,1)} custom-call(f32[1024,16]{1,0:T(8,128)} %get-tuple-element.26.a_re, f32[1024,16]{1,0:T(8,128)} %get-tuple-element.25.a_im, f32[1024,128]{1,0:T(8,128)} %get-tuple-element.30.b_re, f32[1024,128]{1,0:T(8,128)} %get-tuple-element.29.b_im), custom_call_target="tpu_custom_call" | custom-call | flops 16777216 | bytes 8388608 | tf_op jit(solution)/shard_map/chirp/pallas_call | solution.py:305
  87.6 6.7 %rows.2 = bf16[8,2,2,128,128]{4,3,2,1,0:T(8,128)(2,1)} custom-call(f32[2,4]{1,0:T(2,128)} %pad_maximum_fusion.5.mix, bf16[8,2,128,2048]{3,2,1,0:T(8,128)(2,1)} %chirp.2.tab, bf16[8,256,256]{2,1,0:T(8,128)(2,1)} %copy-done.1), custom_call_target="tpu_custom_call" | custom-call | tf_op jit(solution)/shard_map/rows/pallas_call | solution.py:384
  94.3 4.2 %all-to-all-start.1 = ((bf16[8,2,2,128,128]{4,3,2,1,0:T(8,128)(2,1)}), bf16[8,2,2,128,128]{4,3,2,1,0:T(8,128)(2,1)S(1)}, u32[]{:S(2)}, u32[]{:S(2)}) async-start(bf16[8,2,2,128,128]{4,3,2,1,0:T(8,128)(2,1)} %rows.2), calls=%async_computation.1 | async-start | bytes 2097152 | tf_op jit(solution)/shard_map/all_to_all | solution.py:397
  98.8 1.9 sine_negate_fusion.2
  102.4 3.8 %chirp.3.tab = bf16[1,2,512,1024]{3,2,1,0:T(8,128)(2,1)} custom-call(f32[512,8]{1,0:T(8,128)} %get-tuple-element.28.a_re, f32[512,8]{1,0:T(8,128)} %get-tuple-element.27.a_im, f32[512,128]{1,0:T(8,128)} %get-tuple-element.32.b_re, f32[512,128]{1,0:T(8,128)} %get-tuple-element.31.b_im), custom_call_target="tpu_custom_call" | custom-call | flops 4194304 | bytes 2097152 | tf_op jit(solution)/shard_map/chirp/pallas_call | solution.py:305
  106.2 7.7 %all-to-all-done.1.g = bf16[8,2,2,128,128]{4,3,2,1,0:T(8,128)(2,1)S(1)} async-done(((bf16[8,2,2,128,128]{4,3,2,1,0:T(8,128)(2,1)}), bf16[8,2,2,128,128]{4,3,2,1,0:T(8,128)(2,1)S(1)}, u32[]{:S(2)}, u32[]{:S(2)}) %all-to-all-start.1) | async-done | bytes 1048608 | tf_op jit(solution)/shard_map/all_to_all | solution.py:397
  114.9 6.0 %cols.2 = bf16[4,4,2,128,256]{4,3,2,1,0:T(8,128)(2,1)} custom-call(bf16[8,2,2,128,128]{4,3,2,1,0:T(8,128)(2,1)} %copy-done.3, bf16[1,2,512,1024]{3,2,1,0:T(8,128)(2,1)} %chirp.3.tab), custom_call_target="tpu_custom_call" | custom-call | flops 4294967296 | bytes 2097152 | tf_op jit(solution)/shard_map/cols/pallas_call | solution.py:398
  122.1 18.4 %all_to_all.20.v = bf16[8,256,256]{2,1,0:T(8,128)(2,1)} all-to-all(bf16[8,256,256]{2,1,0:T(8,128)(2,1)S(1)} %copy-done.2), channel_id=1, replica_groups=mesh['gx'=8,'gy'=4] {'gx'}, dimensions={0} | all-to-all | bytes 2097152 | tf_op jit(solution)/shard_map/all_to_all | solution.py:383
  140.6 6.8 %rows.3 = bf16[8,2,2,128,128]{4,3,2,1,0:T(8,128)(2,1)} custom-call(f32[2,4]{1,0:T(2,128)} %pad_maximum_fusion.5.mix, bf16[8,2,128,2048]{3,2,1,0:T(8,128)(2,1)} %chirp.2.tab, bf16[8,256,256]{2,1,0:T(8,128)(2,1)} %all_to_all.20.v), custom_call_target="tpu_custom_call" | custom-call | tf_op jit(solution)/shard_map/rows/pallas_call | solution.py:384
  147.3 19.6 %all_to_all.21.g = bf16[8,2,2,128,128]{4,3,2,1,0:T(8,128)(2,1)} all-to-all(bf16[8,2,2,128,128]{4,3,2,1,0:T(8,128)(2,1)} %rows.3), channel_id=1, replica_groups=mesh['gx'=8,'gy'=4] {'gx'}, dimensions={0} | all-to-all | bytes 2097152 | tf_op jit(solution)/shard_map/all_to_all | solution.py:397
  166.9 6.0 %cols.3 = bf16[4,4,2,128,256]{4,3,2,1,0:T(8,128)(2,1)} custom-call(bf16[8,2,2,128,128]{4,3,2,1,0:T(8,128)(2,1)} %all_to_all.21.g, bf16[1,2,512,1024]{3,2,1,0:T(8,128)(2,1)} %chirp.3.tab), custom_call_target="tpu_custom_call" | custom-call | flops 4294967296 | bytes 2097152 | tf_op jit(solution)/shard_map/cols/pallas_call | solution.py:398
  174.1 40.9 %reduce-scatter.5.cloned.1.call-done = bf16[1,4,2,128,256]{4,3,2,1,0:T(8,128)(2,1)} async-done(((bf16[4,4,2,128,256]{4,3,2,1,0:T(8,128)(2,1)}), bf16[1,4,2,128,256]{4,3,2,1,0:T(8,128)(2,1)}) %reduce-scatter.5.cloned.1.call-update) | async-done | bytes 524304 | tf_op jit(solution)/shard_map/reduce_scatter | solution.py:414
  216.4 2.9 %copy.42 = f32[128,2,4,2,256]{4,3,2,1,0:T(2,128)} copy(f32[128,2,4,2,256]{4,0,3,2,1:T(8,128)S(1)} %pad_maximum_fusion.1) | data formatting | bytes 4194304 | tf_op jit(solution)/shard_map/concatenate | solution.py:417
  (61 shorter events, 20.9 us)
Async XLA Ops:
  13.2 12.1 %copy-start.4 = (f32[2]{0:T(128)S(1)}, f32[2]{0:T(128)}, u32[]{:S(2)}) copy-start(f32[2]{0:T(128)} %param.13) | copy-start | bytes 28
  15.4 10.5 %collective-permute-start = (f32[21,2,256]{2,1,0:T(2,128)S(1)}, f32[21,2,256]{2,1,0:T(2,128)S(1)}, u32[]{:S(2)}, u32[]{:S(2)}) collective-permute-start(f32[21,2,256]{2,1,0:T(2,128)S(1)} %maximum_bitcast_fusion), channel_id=1, source_target_pairs={{1,0},{2,1},{3,2},{5,4},{6,5},{7,6},{9,8},{10,9},{11,10},{13,12},{... | collective-permute-start | bytes 129032 | tf_op jit(solution)/shard_map/ppermute | solution.py:36
  17.6 10.6 %collective-permute-start.1 = (f32[21,2,256]{2,1,0:T(2,128)S(1)}, f32[21,2,256]{2,1,0:T(2,128)S(1)}, u32[]{:S(2)}, u32[]{:S(2)}) collective-permute-start(f32[21,2,256]{2,1,0:T(2,128)S(1)} %maximum_bitcast_fusion.1), channel_id=1, source_target_pairs={{0,1},{1,2},{2,3},{4,5},{5,6},{6,7},{8,9},{9,10},{10,11},{12,13},{... | collective-permute-start | bytes 129032 | tf_op jit(solution)/shard_map/ppermute | solution.py:36
  34.0 6.5 %copy-start = (f32[21,256,128]{2,1,0:T(8,128)}, f32[21,256,128]{2,1,0:T(8,128)S(1)}, u32[]{:S(2)}) copy-start(f32[21,256,128]{2,1,0:T(8,128)S(1)} %pad_maximum_fusion.colh) | copy-start | bytes 8257540
  34.1 4.4 %collective-permute-start.2 = (f32[21,2,640]{2,1,0:T(2,128)S(1)}, f32[21,2,640]{2,1,0:T(2,128)S(1)}, u32[]{:S(2)}, u32[]{:S(2)}) collective-permute-start(f32[21,2,640]{2,1,0:T(2,128)S(1)} %pad_maximum_fusion.3), channel_id=1, source_target_pairs={{4,0},{8,4},{12,8},{16,12},{20,16},{24,20},{28,24},{5,1},{9,5},{13... | collective-permute-start | bytes 322568 | tf_op jit(solution)/shard_map/ppermute | solution.py:36
  35.5 4.0 %collective-permute-start.3 = (f32[21,2,640]{2,1,0:T(2,128)S(1)}, f32[21,2,640]{2,1,0:T(2,128)S(1)}, u32[]{:S(2)}, u32[]{:S(2)}) collective-permute-start(f32[21,2,640]{2,1,0:T(2,128)S(1)} %pad_maximum_fusion.4), channel_id=1, source_target_pairs={{0,4},{4,8},{8,12},{12,16},{16,20},{20,24},{24,28},{1,5},{5,9},{9,... | collective-permute-start | bytes 322568 | tf_op jit(solution)/shard_map/ppermute | solution.py:36
  63.2 23.4 %all-to-all-start = ((bf16[8,256,256]{2,1,0:T(8,128)(2,1)}), bf16[8,256,256]{2,1,0:T(8,128)(2,1)S(1)}, u32[]{:S(2)}, u32[]{:S(2)}) async-start(bf16[8,256,256]{2,1,0:T(8,128)(2,1)} %get-tuple-element.9), calls=%async_computation | async-start | bytes 2097152 | tf_op jit(solution)/shard_map/all_to_all | solution.py:383
  86.6 1.0 copy-start.1
  94.3 19.6 %all-to-all-start.1 = ((bf16[8,2,2,128,128]{4,3,2,1,0:T(8,128)(2,1)}), bf16[8,2,2,128,128]{4,3,2,1,0:T(8,128)(2,1)S(1)}, u32[]{:S(2)}, u32[]{:S(2)}) async-start(bf16[8,2,2,128,128]{4,3,2,1,0:T(8,128)(2,1)} %rows.2), calls=%async_computation.1 | async-start | bytes 2097152 | tf_op jit(solution)/shard_map/all_to_all | solution.py:397
  98.5 74.5 %reduce-scatter.3.cloned.1.call-start = ((), (), s32[]{:S(2)}) async-start(), calls=%async_computation.6 | async-start | bytes 2621440 | tf_op jit(solution)/shard_map/reduce_scatter | solution.py:414
  113.9 1.0 copy-start.3
  120.9 1.2 copy-start.2
  121.0 94.1 %reduce-scatter.5.cloned.1.call-start = ((), (), s32[]{:S(2)}) async-start(), calls=%async_computation.7 | async-start | bytes 2621440 | tf_op jit(solution)/shard_map/reduce_scatter | solution.py:414
Sparse Core Ops, SparseCore 0:
  121.1 41.9 reduce-scatter.2
  173.1 41.9 reduce-scatter.4

commit v4 on v3

--- a/solution.py
+++ b/solution.py
@@ -39,9 +39,9 @@
 def yee_kernel(
     grid_rows, grid_cols, gx,
     e_hbm, h_hbm, m_hbm, colh, rowh, eps, pos, amp,
-    e_out, h_out, *rest,
+    e_out, h_out, sd_out,
+    e_ext, h_ext, m_main, scale, src, first, sems,
 ):
-    sd_outs, (e_ext, h_ext, m_main, scale, src, first, sems) = rest[:SETS], rest[SETS:]
     rows, cols = m_main.shape[1:]
     width = cols + PAD
     high = e_ext.shape[1]
@@ -191,14 +191,16 @@
                 for item, face in enumerate(faces):
                     if last:
                         old = first[item, now, :]
-                        here = pl.ds(r - BASE, CHUNK)
+                        here = pl.ds(
+                            pl.multiple_of(r - BASE + item // EACH * rows, CHUNK), CHUNK
+                        )
                         span = cols // gx
                         place = (item % EACH) * span
                         for which, value in enumerate((old + face, face - old)):
                             lo = which * EACH * span + place
                             for j in range(gx):
                                 piece = value[:, j * span : (j + 1) * span].astype(jnp.bfloat16)
-                                sd_outs[item // EACH][j, here, lo : lo + span] = piece
+                                sd_out[j, here, lo : lo + span] = piece
                     else:
                         first[item, now, :] = face
         return carry
@@ -257,9 +259,9 @@
             jax.ShapeDtypeStruct((planes, rows, cols), f32),
             jax.ShapeDtypeStruct((planes, rows, cols), f32),
         )
-        + (jax.ShapeDtypeStruct((gx, rows, 2 * EACH * (cols // gx)), jnp.bfloat16),) * SETS,
+        + (jax.ShapeDtypeStruct((gx, SETS * rows, 2 * EACH * (cols // gx)), jnp.bfloat16),),
         in_specs=[ANY, ANY, ANY, VM, VM, SM, VM, VM],
-        out_specs=(ANY, ANY) + (VM,) * SETS,
+        out_specs=(ANY, ANY, VM),
         scratch_shapes=[
             pltpu.VMEM((planes, high, width), f32),
             pltpu.VMEM((planes, high, width), f32),
@@ -315,7 +317,7 @@
     )(a_re, a_im, b_re, b_im)
 
 
-def rows_kernel(mix, tab, v, out):
+def rows_kernel(mix, tab, v, *outs):
     group, _, nu, depth = tab.shape
     half = v.shape[2] // 2
     left = tab[...].reshape(group * 2 * nu, depth)
@@ -329,30 +331,28 @@
             p_re, p_im, q_re, q_im = (mix[f, i] for i in range(4))
             re = p_re * s_re - p_im * s_im + (q_re * d_re - q_im * d_im)
             im = p_re * s_im + p_im * s_re + (q_re * d_im + q_im * d_re)
-            out[b, f, 0] = re.astype(jnp.bfloat16)
-            out[b, f, 1] = im.astype(jnp.bfloat16)
+            outs[f][b, 0] = re.astype(jnp.bfloat16)
+            outs[f][b, 1] = im.astype(jnp.bfloat16)
 
 
 def cols_kernel(g, tab, out, left):
-    gx, _, _, nu, wide = g.shape
+    gx, _, nu, wide = g.shape
     span = wide // EACH
 
     @pl.when(pl.program_id(0) == 0)
     def _():
-        for f in range(NF):
-            for c in range(2):
-                got = [g[j, f, c].astype(jnp.float32) for j in range(gx)]
-                for k in range(EACH):
-                    at = (f * EACH + k) * nu
-                    row = [piece[:, k * span : (k + 1) * span] for piece in got]
-                    left[c, at : at + nu, :] = jnp.concatenate(row, 1).astype(jnp.bfloat16)
+        for c in range(2):
+            got = [g[j, c].astype(jnp.float32) for j in range(gx)]
+            for k in range(EACH):
+                row = [piece[:, k * span : (k + 1) * span] for piece in got]
+                left[c, k * nu : (k + 1) * nu, :] = jnp.concatenate(row, 1).astype(jnp.bfloat16)
 
     y_re = tab[0, 0]
     y_im = tab[0, 1]
     dot = functools.partial(jnp.dot, preferred_element_type=jnp.float32)
     re = dot(left[0], y_re) - dot(left[1], y_im)
     im = dot(left[0], y_im) + dot(left[1], y_re)
-    for i in range(NF * EACH):
+    for i in range(EACH):
         out[0, i, 0] = re[i * nu : (i + 1) * nu].astype(out.dtype)
         out[0, i, 1] = im[i * nu : (i + 1) * nu].astype(out.dtype)
 
@@ -370,7 +370,7 @@
     x_tab = table(angle_index - NA // 2, 0, grid_rows, zoom_factor * grid_rows, gx)
     y_cells = col_start + jnp.arange(cols, dtype=jnp.int32)
     y_tab = table(y_cells, NA // 4, NA, zoom_factor * grid_cols, 1)
-    e_new, h_new, *sd = yee(e_field, h_field, material, eps_table, src_pos, src_amp)
+    e_new, h_new, sd = yee(e_field, h_field, material, eps_table, src_pos, src_amp)
     turn_re, turn_im = jnp.cos(1.5 * freqs), jnp.sin(1.5 * freqs)
     half_re, half_im = jnp.cos(0.5 * freqs), jnp.sin(0.5 * freqs)
     mix = jnp.stack(
@@ -378,43 +378,51 @@
     )
     group = 2
     inv_norm = 1.0 / math.sqrt(grid_rows * grid_cols)
+    got = lax.all_to_all(sd, "gx", split_axis=0, concat_axis=0, tiled=True)
     fars = []
-    for sent in sd:
-        got = lax.all_to_all(sent, "gx", split_axis=0, concat_axis=0, tiled=True)
-        g = pl.pallas_call(
+    for group_at in range(SETS):
+        halves = pl.pallas_call(
             rows_kernel,
             grid=(gx // group,),
-            out_shape=jax.ShapeDtypeStruct((gx, NF, 2, nu, wide), bf16),
+            out_shape=[jax.ShapeDtypeStruct((gx, 2, nu, wide), bf16)] * NF,
             in_specs=[
                 SM,
                 pl.BlockSpec((group, 2, nu, grid_rows), lambda i: (i, 0, 0, 0)),
-                pl.BlockSpec((gx, rows, 2 * wide), lambda i: (0, 0, 0)),
+                pl.BlockSpec((gx, rows, 2 * wide), lambda i, at=group_at: (0, at, 0)),
             ],
-            out_specs=pl.BlockSpec((group, NF, 2, nu, wide), lambda i: (i, 0, 0, 0, 0)),
+            out_specs=[pl.BlockSpec((group, 2, nu, wide), lambda i: (i, 0, 0, 0))] * NF,
             compiler_params=pltpu.CompilerParams(vmem_limit_bytes=BIG),
+            cost_estimate=pl.CostEstimate(
+                flops=8 * NA * grid_rows * wide,
+                bytes_accessed=4 * NA * grid_rows,
+                transcendentals=0,
+            ),
             name="rows",
         )(mix, x_tab, got)
-        moved = lax.all_to_all(g, "gx", split_axis=0, concat_axis=0, tiled=True)
-        share = pl.pallas_call(
-            cols_kernel,
-            grid=(gy,),
-            out_shape=jax.ShapeDtypeStruct((gy, NF * EACH, 2, nu, vb), bf16),
-            in_specs=[
-                pl.BlockSpec((gx, NF, 2, nu, wide), lambda j: (0, 0, 0, 0, 0)),
-                pl.BlockSpec((1, 2, cols, vb), lambda j: (0, 0, 0, j)),
-            ],
-            out_specs=pl.BlockSpec((1, NF * EACH, 2, nu, vb), lambda j: (j, 0, 0, 0, 0)),
-            scratch_shapes=[pltpu.VMEM((2, NF * EACH * nu, cols), bf16)],
-            compiler_params=pltpu.CompilerParams(vmem_limit_bytes=BIG),
-            cost_estimate=pl.CostEstimate(
-                flops=16 * NF * EACH * nu * cols * NA, bytes_accessed=16 * nu * NA, transcendentals=0
-            ),
-            name="cols",
-        )(moved, y_tab)
-        summed = lax.psum_scatter(share, "gy", scatter_dimension=0, tiled=True)
-        scaled = summed[0].astype(jnp.float32) * inv_norm
-        fars.append(jnp.transpose(scaled, (2, 0, 1, 3)).reshape(nu, NF, EACH, 2, vb))
-    far = jnp.concatenate(fars, 2).reshape(nu, NF * 4, 2, vb)
+        done = []
+        for g in halves:
+            moved = lax.all_to_all(g, "gx", split_axis=0, concat_axis=0, tiled=True)
+            share = pl.pallas_call(
+                cols_kernel,
+                grid=(gy,),
+                out_shape=jax.ShapeDtypeStruct((gy, EACH, 2, nu, vb), bf16),
+                in_specs=[
+                    pl.BlockSpec((gx, 2, nu, wide), lambda j: (0, 0, 0, 0)),
+                    pl.BlockSpec((1, 2, cols, vb), lambda j: (0, 0, 0, j)),
+                ],
+                out_specs=pl.BlockSpec((1, EACH, 2, nu, vb), lambda j: (j, 0, 0, 0, 0)),
+                scratch_shapes=[pltpu.VMEM((2, EACH * nu, cols), bf16)],
+                compiler_params=pltpu.CompilerParams(vmem_limit_bytes=BIG),
+                cost_estimate=pl.CostEstimate(
+                    flops=8 * EACH * nu * cols * NA, bytes_accessed=16 * nu * NA, transcendentals=0
+                ),
+                name="cols",
+            )(moved, y_tab)
+            summed = lax.psum_scatter(share, "gy", scatter_dimension=0, tiled=True)
+            scaled = summed[0].astype(jnp.float32) * inv_norm
+            done.append(jnp.transpose(scaled, (2, 0, 1, 3)))
+        fars.append(done)
+    far = jnp.concatenate([fars[at][f] for f in range(NF) for at in range(SETS)], 1)
     shape = e_field.shape
     return (e_new.reshape(shape), h_new.reshape(shape), far)
 

time: 228 us -> 246 us (1.079)
  waiting for transfers between devices: 49.6 us -> 59.3 us
  Pallas kernels: 61.4 us -> 68.7 us
    all_to_all x1 -> x3, blocking collectives: 19.6 us -> 39.5 us  [on_device(): moved = lax.all_to_all(g, 'gx', split_axis=0, concat_axis=0, tiled=True)]
    all_to_all x1 -> x0, blocking collectives: 18.4 us -> none  [on_device(): got = lax.all_to_all(sent, 'gx', split_axis=0, concat_axis=0, tiled=True)]
    all_to_all x1, waiting for transfers between devices: 0.01 us -> 9.64 us  [on_device(): got = lax.all_to_all(sd, 'gx', split_axis=0, concat_axis=0, tiled=True)]
    pallas_call x2 -> x4, Pallas kernels: 12.1 us -> 19.3 us  [on_device(): pl.pallas_call(cols_kernel, grid=(gy,), out_shape=jax.ShapeDtypeStruct((g...]
    reduce_scatter x2 -> x4, waiting for transfers between devices: 41 us -> 46.7 us  [on_device(): summed = lax.psum_scatter(share, 'gy', scatter_dimension=0, tiled=True)]
    all_to_all x1, waiting for transfers between devices: 7.69 us -> 2.12 us  [on_device(): moved = lax.all_to_all(g, 'gx', split_axis=0, concat_axis=0, tiled=True)]
    transpose x0 -> x4, other arithmetic: none -> 3.96 us  [on_device(): done.append(jnp.transpose(scaled, (2, 0, 1, 3)))]
    concatenate x1 -> x0, local copies, waits for them, and re-layouts: 2.94 us -> none  [on_device(): far = jnp.concatenate(fars, 2).reshape(nu, NF * 4, 2, vb)]
  transfers between devices with their start and end apart: 8 -> 10, of which waited for: 3 -> 5; matrix products, arithmetic and copies ran while one was open for 8% -> 8% of each run, Pallas kernels for 11% -> 14%
where the time goes in v4:
time: 246 us; the launch traced here: 245 us
  Pallas kernels  68.7 us (28%)
  waiting for transfers between devices  59.3 us (24%)
  blocking collectives  39.5 us (16%)
  starting transfers between devices  22 us (9%)
  other arithmetic  20.8 us (8%)
  local copies, waits for them, and re-layouts  20.2 us (8%)
  between operations  14 us (6%)
    reduce_scatter x4, waiting for transfers between devices, on_device(): summed = lax.psum_scatter(share, 'gy', scatter_dimension=0, tiled=True)  46.7 us
    all_to_all x3, blocking collectives, on_device(): moved = lax.all_to_all(g, 'gx', split_axis=0, concat_axis=0, tiled=True)  39.5 us
    pallas_call x1, Pallas kernels, yee(): pl.pallas_call(functools.partial(yee_kernel, grid_rows, grid_cols, gx), o...  22.7 us
    pallas_call x4, Pallas kernels, on_device(): pl.pallas_call(cols_kernel, grid=(gy,), out_shape=jax.ShapeDtypeStruct((g...  19.3 us
    pallas_call x2, Pallas kernels, on_device(): pl.pallas_call(rows_kernel, grid=(gx // group,), out_shape=[jax.ShapeDtyp...  13.6 us
    pallas_call x2, Pallas kernels, table(): pl.pallas_call(table_kernel, grid=(blocks,), out_shape=jax.ShapeDtypeStru...  13.1 us
    ppermute x4, starting transfers between devices, shifted(): return lax.ppermute(block, axis, route)  11.2 us
    neg x4, other arithmetic, unit(): return (jnp.cos(angle), -jnp.sin(angle))  9.64 us
  transfers between devices with their start and end apart: 10, of which 5 were waited for; matrix products, arithmetic and copies ran while one was open for 8% of the time, Pallas kernels for 14%

profile of v4, /device:TPU:0, one launch (start us, length us, event | category | flops | bytes accessed | tf_op | source)
XLA Modules:
  0.0 244.6 jit_solution(1027347841100580655)
XLA Ops:
  17.6 5.6 %collective-permute-start.1 = (f32[21,2,256]{2,1,0:T(2,128)S(1)}, f32[21,2,256]{2,1,0:T(2,128)S(1)}, u32[]{:S(2)}, u32[]{:S(2)}) collective-permute-start(f32[21,2,256]{2,1,0:T(2,128)S(1)} %maximum_bitcast_fusion.1), channel_id=1, source_target_pairs={{0,1},{1,2},{2,3},{4,5},{5,6},{6,7},{8,9},{9,10},{10,11},{12,13},{... | collective-permute-start | bytes 129032 | tf_op jit(solution)/shard_map/ppermute | solution.py:36
  25.3 2.4 copy.31
  30.1 3.4 %pad_maximum_fusion.colh = f32[21,256,128]{2,1,0:T(8,128)S(1)} fusion(f32[21,256,2]{2,1,0:T(8,128)} %bitcast.37, f32[21,256,2]{2,1,0:T(8,128)} %bitcast.36, f32[128]{0:T(128)S(1)} %pad.20.clone), kind=kLoop, calls=%fused_computation | loop fusion | flops 1376256 | bytes 2839040 | tf_op jit(solution)/shard_map/concatenate | solution.py:243
  34.9 3.0 %collective-permute-start.3 = (f32[21,2,640]{2,1,0:T(2,128)S(1)}, f32[21,2,640]{2,1,0:T(2,128)S(1)}, u32[]{:S(2)}, u32[]{:S(2)}) collective-permute-start(f32[21,2,640]{2,1,0:T(2,128)S(1)} %pad_maximum_fusion.4), channel_id=1, source_target_pairs={{0,4},{4,8},{8,12},{12,16},{16,20},{20,24},{24,28},{1,5},{5,9},{9,... | collective-permute-start | bytes 322568 | tf_op jit(solution)/shard_map/ppermute | solution.py:36
  39.9 22.7 %yee.1 = (f32[9,256,512]{2,1,0:T(8,128)}, f32[9,256,512]{2,1,0:T(8,128)}, bf16[8,512,256]{2,1,0:T(8,128)(2,1)}) custom-call(f32[9,256,512]{2,1,0:T(8,128)} %bitcast.40, f32[9,256,512]{2,1,0:T(8,128)} %bitcast.43, s32[3,256,512]{2,1,0:T(8,128)} %m_hbm.1, f32[21,256,128]{2,1,0:T(8,128)} %copy-done.1, f32[21,16,640]{2,1,0:T(8,128)} %pad_maximum_fusion.2.rowh, ...), custom_call_target="tpu_custom_call" | custom-call | tf_op jit(solution)/shard_map/yee/pallas_call | solution.py:256
  62.6 7.1 %all-to-all-start = ((bf16[8,512,256]{2,1,0:T(8,128)(2,1)}), bf16[8,512,256]{2,1,0:T(8,128)(2,1)S(1)}, u32[]{:S(2)}, u32[]{:S(2)}) async-start(bf16[8,512,256]{2,1,0:T(8,128)(2,1)} %get-tuple-element.12), calls=%async_computation | async-start | bytes 4194304 | tf_op jit(solution)/shard_map/all_to_all | solution.py:381
  70.8 3.3 %sine_negate_fusion = (f32[1024,128]{1,0:T(8,128)}, f32[1024,128]{1,0:T(8,128)}) fusion(s32[1024]{0:T(1024)S(1)} %iota_add_fusion), kind=kLoop, calls=%fused_computation.13 | loop fusion | flops 1966080 | bytes 1052672 | tf_op jit(solution)/shard_map/neg | solution.py:295
  74.0 2.8 %sine_negate_fusion.1 = (f32[1024,16]{1,0:T(8,128)}, f32[1024,16]{1,0:T(8,128)}) fusion(f32[1024,16]{1,0:T(8,128)S(1)} %copy.40), kind=kLoop, calls=%fused_computation.16 | loop fusion | flops 32768 | bytes 196608 | tf_op jit(solution)/shard_map/neg | solution.py:295
  76.8 9.3 %chirp.2.tab = bf16[8,2,128,2048]{3,2,1,0:T(8,128)(2,1)} custom-call(f32[1024,16]{1,0:T(8,128)} %get-tuple-element.41.a_re, f32[1024,16]{1,0:T(8,128)} %get-tuple-element.40.a_im, f32[1024,128]{1,0:T(8,128)} %get-tuple-element.45.b_re, f32[1024,128]{1,0:T(8,128)} %get-tuple-element.44.b_im), custom_call_target="tpu_custom_call" | custom-call | flops 16777216 | bytes 8388608 | tf_op jit(solution)/shard_map/chirp/pallas_call | solution.py:307
  86.8 9.6 %all-to-all-done.v = bf16[8,512,256]{2,1,0:T(8,128)(2,1)S(1)} async-done(((bf16[8,512,256]{2,1,0:T(8,128)(2,1)}), bf16[8,512,256]{2,1,0:T(8,128)(2,1)S(1)}, u32[]{:S(2)}, u32[]{:S(2)}) %all-to-all-start) | async-done | bytes 2097184 | tf_op jit(solution)/shard_map/all_to_all | solution.py:381
  97.7 6.8 %rows.2 = (bf16[8,2,128,128]{3,2,1,0:T(8,128)(2,1)}, bf16[8,2,128,128]{3,2,1,0:T(8,128)(2,1)}) custom-call(f32[2,4]{1,0:T(2,128)} %pad_maximum_fusion.5.mix, bf16[8,2,128,2048]{3,2,1,0:T(8,128)(2,1)} %chirp.2.tab, bf16[8,512,256]{2,1,0:T(8,128)(2,1)} %copy-done), custom_call_target="tpu_custom_call" | custom-call | flops 2147483648 | bytes 8388608 | tf_op jit(solution)/shard_map/rows/pallas_call | solution.py:384
  104.5 3.5 %all-to-all-start.1 = ((bf16[8,2,128,128]{3,2,1,0:T(8,128)(2,1)}), bf16[8,2,128,128]{3,2,1,0:T(8,128)(2,1)S(1)}, u32[]{:S(2)}, u32[]{:S(2)}) async-start(bf16[8,2,128,128]{3,2,1,0:T(8,128)(2,1)} %get-tuple-element.13), calls=%async_computation.1 | async-start | bytes 1048576 | tf_op jit(solution)/shard_map/all_to_all | solution.py:404
  111.6 3.9 %chirp.3.tab = bf16[1,2,512,1024]{3,2,1,0:T(8,128)(2,1)} custom-call(f32[512,8]{1,0:T(8,128)} %get-tuple-element.43.a_re, f32[512,8]{1,0:T(8,128)} %get-tuple-element.42.a_im, f32[512,128]{1,0:T(8,128)} %get-tuple-element.47.b_re, f32[512,128]{1,0:T(8,128)} %get-tuple-element.46.b_im), custom_call_target="tpu_custom_call" | custom-call | flops 4194304 | bytes 2097152 | tf_op jit(solution)/shard_map/chirp/pallas_call | solution.py:307
  118.4 4.8 %cols.4 = bf16[4,2,2,128,256]{4,3,2,1,0:T(8,128)(2,1)} custom-call(bf16[8,2,128,128]{3,2,1,0:T(8,128)(2,1)} %copy-done.3, bf16[1,2,512,1024]{3,2,1,0:T(8,128)(2,1)} %chirp.3.tab), custom_call_target="tpu_custom_call" | custom-call | flops 1073741824 | bytes 2097152 | tf_op jit(solution)/shard_map/cols/pallas_call | solution.py:405
  123.3 12.8 %all_to_all.25.g = bf16[8,2,128,128]{3,2,1,0:T(8,128)(2,1)} all-to-all(bf16[8,2,128,128]{3,2,1,0:T(8,128)(2,1)S(1)} %copy-done.2), channel_id=1, replica_groups=mesh['gx'=8,'gy'=4] {'gx'}, dimensions={0} | all-to-all | bytes 1048576 | tf_op jit(solution)/shard_map/all_to_all | solution.py:404
  136.1 4.8 %cols.6 = bf16[4,2,2,128,256]{4,3,2,1,0:T(8,128)(2,1)} custom-call(bf16[8,2,128,128]{3,2,1,0:T(8,128)(2,1)} %all_to_all.25.g, bf16[1,2,512,1024]{3,2,1,0:T(8,128)(2,1)} %chirp.3.tab), custom_call_target="tpu_custom_call" | custom-call | flops 1073741824 | bytes 2097152 | tf_op jit(solution)/shard_map/cols/pallas_call | solution.py:405
  141.0 6.8 %rows.3 = (bf16[8,2,128,128]{3,2,1,0:T(8,128)(2,1)}, bf16[8,2,128,128]{3,2,1,0:T(8,128)(2,1)}) custom-call(f32[2,4]{1,0:T(2,128)} %pad_maximum_fusion.5.mix, bf16[8,2,128,2048]{3,2,1,0:T(8,128)(2,1)} %chirp.2.tab, bf16[8,512,256]{2,1,0:T(8,128)(2,1)} %copy-done), custom_call_target="tpu_custom_call" | custom-call | flops 2147483648 | bytes 8388608 | tf_op jit(solution)/shard_map/rows/pallas_call | solution.py:384
  147.8 13.8 %all_to_all.26.g = bf16[8,2,128,128]{3,2,1,0:T(8,128)(2,1)} all-to-all(bf16[8,2,128,128]{3,2,1,0:T(8,128)(2,1)} %get-tuple-element.14), channel_id=1, replica_groups=mesh['gx'=8,'gy'=4] {'gx'}, dimensions={0} | all-to-all | bytes 1048576 | tf_op jit(solution)/shard_map/all_to_all | solution.py:404
  161.7 4.9 %cols.5 = bf16[4,2,2,128,256]{4,3,2,1,0:T(8,128)(2,1)} custom-call(bf16[8,2,128,128]{3,2,1,0:T(8,128)(2,1)} %all_to_all.26.g, bf16[1,2,512,1024]{3,2,1,0:T(8,128)(2,1)} %chirp.3.tab), custom_call_target="tpu_custom_call" | custom-call | flops 1073741824 | bytes 2097152 | tf_op jit(solution)/shard_map/cols/pallas_call | solution.py:405
  166.6 12.8 %all_to_all.27.g = bf16[8,2,128,128]{3,2,1,0:T(8,128)(2,1)} all-to-all(bf16[8,2,128,128]{3,2,1,0:T(8,128)(2,1)S(1)} %copy-done.4), channel_id=1, replica_groups=mesh['gx'=8,'gy'=4] {'gx'}, dimensions={0} | all-to-all | bytes 1048576 | tf_op jit(solution)/shard_map/all_to_all | solution.py:404
  179.5 4.8 %cols.7 = bf16[4,2,2,128,256]{4,3,2,1,0:T(8,128)(2,1)} custom-call(bf16[8,2,128,128]{3,2,1,0:T(8,128)(2,1)} %all_to_all.27.g, bf16[1,2,512,1024]{3,2,1,0:T(8,128)(2,1)} %chirp.3.tab), custom_call_target="tpu_custom_call" | custom-call | flops 1073741824 | bytes 2097152 | tf_op jit(solution)/shard_map/cols/pallas_call | solution.py:405
  186.3 19.1 %reduce-scatter.7.cloned.1.call-done = bf16[1,2,2,128,256]{4,3,2,1,0:T(8,128)(2,1)} async-done(((bf16[4,2,2,128,256]{4,3,2,1,0:T(8,128)(2,1)}), bf16[1,2,2,128,256]{4,3,2,1,0:T(8,128)(2,1)}) %reduce-scatter.7.cloned.1.call-update) | async-done | bytes 262160 | tf_op jit(solution)/shard_map/reduce_scatter | solution.py:421
  206.4 27.5 %reduce-scatter.11.cloned.1.call-done = bf16[1,2,2,128,256]{4,3,2,1,0:T(8,128)(2,1)} async-done(((bf16[4,2,2,128,256]{4,3,2,1,0:T(8,128)(2,1)}), bf16[1,2,2,128,256]{4,3,2,1,0:T(8,128)(2,1)}) %reduce-scatter.11.cloned.1.call-update) | async-done | bytes 262160 | tf_op jit(solution)/shard_map/reduce_scatter | solution.py:421
  235.1 2.9 %copy.42 = f32[128,8,2,256]{3,2,1,0:T(2,128)} copy(f32[128,8,2,256]{3,0,2,1:T(8,128)S(1)} %pad_maximum_fusion.1) | data formatting | bytes 4194304
  (74 shorter events, 32.1 us)
Async XLA Ops:
  15.4 10.0 %collective-permute-start = (f32[21,2,256]{2,1,0:T(2,128)S(1)}, f32[21,2,256]{2,1,0:T(2,128)S(1)}, u32[]{:S(2)}, u32[]{:S(2)}) collective-permute-start(f32[21,2,256]{2,1,0:T(2,128)S(1)} %maximum_bitcast_fusion), channel_id=1, source_target_pairs={{1,0},{2,1},{3,2},{5,4},{6,5},{7,6},{9,8},{10,9},{11,10},{13,12},{... | collective-permute-start | bytes 129032 | tf_op jit(solution)/shard_map/ppermute | solution.py:36
  17.6 10.1 %collective-permute-start.1 = (f32[21,2,256]{2,1,0:T(2,128)S(1)}, f32[21,2,256]{2,1,0:T(2,128)S(1)}, u32[]{:S(2)}, u32[]{:S(2)}) collective-permute-start(f32[21,2,256]{2,1,0:T(2,128)S(1)} %maximum_bitcast_fusion.1), channel_id=1, source_target_pairs={{0,1},{1,2},{2,3},{4,5},{5,6},{6,7},{8,9},{9,10},{10,11},{12,13},{... | collective-permute-start | bytes 129032 | tf_op jit(solution)/shard_map/ppermute | solution.py:36
  33.5 6.5 %copy-start.1 = (f32[21,256,128]{2,1,0:T(8,128)}, f32[21,256,128]{2,1,0:T(8,128)S(1)}, u32[]{:S(2)}) copy-start(f32[21,256,128]{2,1,0:T(8,128)S(1)} %pad_maximum_fusion.colh) | copy-start | bytes 8257540
  33.6 4.5 %collective-permute-start.2 = (f32[21,2,640]{2,1,0:T(2,128)S(1)}, f32[21,2,640]{2,1,0:T(2,128)S(1)}, u32[]{:S(2)}, u32[]{:S(2)}) collective-permute-start(f32[21,2,640]{2,1,0:T(2,128)S(1)} %pad_maximum_fusion.3), channel_id=1, source_target_pairs={{4,0},{8,4},{12,8},{16,12},{20,16},{24,20},{28,24},{5,1},{9,5},{13... | collective-permute-start | bytes 322568 | tf_op jit(solution)/shard_map/ppermute | solution.py:36
  34.9 4.0 %collective-permute-start.3 = (f32[21,2,640]{2,1,0:T(2,128)S(1)}, f32[21,2,640]{2,1,0:T(2,128)S(1)}, u32[]{:S(2)}, u32[]{:S(2)}) collective-permute-start(f32[21,2,640]{2,1,0:T(2,128)S(1)} %pad_maximum_fusion.4), channel_id=1, source_target_pairs={{0,4},{4,8},{8,12},{12,16},{16,20},{20,24},{24,28},{1,5},{5,9},{9,... | collective-permute-start | bytes 322568 | tf_op jit(solution)/shard_map/ppermute | solution.py:36
  62.6 7.1 %copy-start.5 = (f32[2]{0:T(128)S(1)}, f32[2]{0:T(128)}, u32[]{:S(2)}) copy-start(f32[2]{0:T(128)} %param.13) | copy-start | bytes 28
  62.6 33.7 %all-to-all-start = ((bf16[8,512,256]{2,1,0:T(8,128)(2,1)}), bf16[8,512,256]{2,1,0:T(8,128)(2,1)S(1)}, u32[]{:S(2)}, u32[]{:S(2)}) async-start(bf16[8,512,256]{2,1,0:T(8,128)(2,1)} %get-tuple-element.12), calls=%async_computation | async-start | bytes 4194304 | tf_op jit(solution)/shard_map/all_to_all | solution.py:381
  96.4 1.3 copy-start
  104.5 13.1 %all-to-all-start.1 = ((bf16[8,2,128,128]{3,2,1,0:T(8,128)(2,1)}), bf16[8,2,128,128]{3,2,1,0:T(8,128)(2,1)S(1)}, u32[]{:S(2)}, u32[]{:S(2)}) async-start(bf16[8,2,128,128]{3,2,1,0:T(8,128)(2,1)} %get-tuple-element.13), calls=%async_computation.1 | async-start | bytes 1048576 | tf_op jit(solution)/shard_map/all_to_all | solution.py:404
  108.0 76.3 %reduce-scatter.5.cloned.1.call-start = ((), (), s32[]{:S(2)}) async-start(), calls=%async_computation.9 | async-start | bytes 1310720 | tf_op jit(solution)/shard_map/reduce_scatter | solution.py:421
  115.5 7.8 %copy-start.2 = (bf16[8,2,128,128]{3,2,1,0:T(8,128)(2,1)S(1)}, bf16[8,2,128,128]{3,2,1,0:T(8,128)(2,1)}, u32[]{:S(2)}) copy-start(bf16[8,2,128,128]{3,2,1,0:T(8,128)(2,1)} %get-tuple-element.15) | copy-start | bytes 1572868
  117.6 0.8 copy-start.3
  123.3 62.1 %reduce-scatter.9.cloned.1.call-start = ((), (), s32[]{:S(2)}) async-start(), calls=%async_computation.11 | async-start | bytes 1310720 | tf_op jit(solution)/shard_map/reduce_scatter | solution.py:421
  141.0 64.4 %reduce-scatter.7.cloned.1.call-start = ((), (), s32[]{:S(2)}) async-start(), calls=%async_computation.10 | async-start | bytes 1310720 | tf_op jit(solution)/shard_map/reduce_scatter | solution.py:421
  161.7 5.0 %copy-start.4 = (bf16[8,2,128,128]{3,2,1,0:T(8,128)(2,1)S(1)}, bf16[8,2,128,128]{3,2,1,0:T(8,128)(2,1)}, u32[]{:S(2)}) copy-start(bf16[8,2,128,128]{3,2,1,0:T(8,128)(2,1)} %get-tuple-element.16) | copy-start | bytes 1572868
  166.6 67.3 %reduce-scatter.11.cloned.1.call-start = ((), (), s32[]{:S(2)}) async-start(), calls=%async_computation.12 | async-start | bytes 1310720 | tf_op jit(solution)/shard_map/reduce_scatter | solution.py:421
Sparse Core Ops, SparseCore 0:
  123.4 25.7 reduce-scatter.4
  151.5 25.7 reduce-scatter.8
  179.6 25.7 reduce-scatter.6
  208.1 25.7 reduce-scatter.10

commit v5 on v3

--- a/solution.py
+++ b/solution.py
@@ -376,7 +376,7 @@
     mix = jnp.stack(
         [turn_re * half_re, turn_im * half_re, -turn_im * half_im, turn_re * half_im], 1
     )
-    group = 2
+    group = 4
     inv_norm = 1.0 / math.sqrt(grid_rows * grid_cols)
     fars = []
     for sent in sd:

time: 228 us -> 226 us (level)
  no operation moved by 1% of the time
where the time goes in v5:
time: 226 us; the launch traced here: 225 us
  Pallas kernels  60 us (27%)
  waiting for transfers between devices  49.6 us (22%)
  blocking collectives  38 us (17%)
  starting transfers between devices  22.6 us (10%)
  local copies, waits for them, and re-layouts  21.2 us (9%)
  other arithmetic  19.1 us (8%)
  between operations  14.3 us (6%)
    reduce_scatter x2, waiting for transfers between devices, on_device(): summed = lax.psum_scatter(share, 'gy', scatter_dimension=0, tiled=True)  41 us
    pallas_call x1, Pallas kernels, yee(): pl.pallas_call(functools.partial(yee_kernel, grid_rows, grid_cols, gx), o...  22.8 us
    all_to_all x1, blocking collectives, on_device(): moved = lax.all_to_all(g, 'gx', split_axis=0, concat_axis=0, tiled=True)  19.6 us
    all_to_all x1, blocking collectives, on_device(): got = lax.all_to_all(sent, 'gx', split_axis=0, concat_axis=0, tiled=True)  18.4 us
    pallas_call x2, Pallas kernels, table(): pl.pallas_call(table_kernel, grid=(blocks,), out_shape=jax.ShapeDtypeStru...  13.1 us
    pallas_call x2, Pallas kernels, on_device(): pl.pallas_call(rows_kernel, grid=(gx // group,), out_shape=jax.ShapeDtype...  12.1 us
    pallas_call x2, Pallas kernels, on_device(): pl.pallas_call(cols_kernel, grid=(gy,), out_shape=jax.ShapeDtypeStruct((g...  12.1 us
    ppermute x4, starting transfers between devices, shifted(): return lax.ppermute(block, axis, route)  11.2 us
  transfers between devices with their start and end apart: 8, of which 3 were waited for; matrix products, arithmetic and copies ran while one was open for 8% of the time, Pallas kernels for 11%

profile of v5, /device:TPU:0, one launch (start us, length us, event | category | flops | bytes accessed | tf_op | source)
XLA Modules:
  0.0 224.8 jit_solution(9341382943639954215)
XLA Ops:
  7.2 2.0 fusion.20
  10.2 2.0 fusion.21
  17.6 5.6 %collective-permute-start.1 = (f32[21,2,256]{2,1,0:T(2,128)S(1)}, f32[21,2,256]{2,1,0:T(2,128)S(1)}, u32[]{:S(2)}, u32[]{:S(2)}) collective-permute-start(f32[21,2,256]{2,1,0:T(2,128)S(1)} %maximum_bitcast_fusion.1), channel_id=1, source_target_pairs={{0,1},{1,2},{2,3},{4,5},{5,6},{6,7},{8,9},{9,10},{10,11},{12,13},{... | collective-permute-start | bytes 129032 | tf_op jit(solution)/shard_map/ppermute | solution.py:36
  25.9 2.4 %copy.31 = f32[21,2,256]{1,2,0:T(8,128)} copy(f32[21,2,256]{2,1,0:T(2,128)S(1)} %collective-permute-done) | data formatting | bytes 86016 | tf_op jit(solution)/shard_map/ppermute | solution.py:36
  28.2 2.4 %copy.35 = f32[21,2,256]{1,2,0:T(8,128)} copy(f32[21,2,256]{2,1,0:T(2,128)S(1)} %collective-permute-done.1) | data formatting | bytes 86016 | tf_op jit(solution)/shard_map/ppermute | solution.py:36
  30.6 3.4 %pad_maximum_fusion.colh = f32[21,256,128]{2,1,0:T(8,128)S(1)} fusion(f32[21,256,2]{2,1,0:T(8,128)} %bitcast.32, f32[21,256,2]{2,1,0:T(8,128)} %bitcast.31, f32[128]{0:T(128)S(1)} %pad.18.clone), kind=kLoop, calls=%fused_computation | loop fusion | flops 1376256 | bytes 2839040 | tf_op jit(solution)/shard_map/concatenate | solution.py:241
  35.5 3.0 %collective-permute-start.3 = (f32[21,2,640]{2,1,0:T(2,128)S(1)}, f32[21,2,640]{2,1,0:T(2,128)S(1)}, u32[]{:S(2)}, u32[]{:S(2)}) collective-permute-start(f32[21,2,640]{2,1,0:T(2,128)S(1)} %pad_maximum_fusion.4), channel_id=1, source_target_pairs={{0,4},{4,8},{8,12},{12,16},{16,20},{20,24},{24,28},{1,5},{5,9},{9,... | collective-permute-start | bytes 322568 | tf_op jit(solution)/shard_map/ppermute | solution.py:36
  40.5 22.8 %yee.1 = (f32[9,256,512]{2,1,0:T(8,128)}, f32[9,256,512]{2,1,0:T(8,128)}, bf16[8,256,256]{2,1,0:T(8,128)(2,1)}, bf16[8,256,256]{2,1,0:T(8,128)(2,1)}) custom-call(f32[9,256,512]{2,1,0:T(8,128)} %bitcast.35, f32[9,256,512]{2,1,0:T(8,128)} %bitcast.38, s32[3,256,512]{2,1,0:T(8,128)} %m_hbm.1, f32[21,256,128]{2,1,0:T(8,128)} %copy-done, ...), custom_call_target="tpu_custom_call" | custom-call | tf_op jit(solution)/shard_map/yee/pallas_call | solution.py:254
  63.2 7.1 %all-to-all-start = ((bf16[8,256,256]{2,1,0:T(8,128)(2,1)}), bf16[8,256,256]{2,1,0:T(8,128)(2,1)S(1)}, u32[]{:S(2)}, u32[]{:S(2)}) async-start(bf16[8,256,256]{2,1,0:T(8,128)(2,1)} %get-tuple-element.9), calls=%async_computation | async-start | bytes 2097152 | tf_op jit(solution)/shard_map/all_to_all | solution.py:383
  70.7 3.3 %sine_negate_fusion = (f32[1024,128]{1,0:T(8,128)}, f32[1024,128]{1,0:T(8,128)}) fusion(s32[1024]{0:T(1024)S(1)} %iota_add_fusion), kind=kLoop, calls=%fused_computation.11 | loop fusion | flops 1966080 | bytes 1052672 | tf_op jit(solution)/shard_map/neg | solution.py:293
  73.9 2.8 %sine_negate_fusion.1 = (f32[1024,16]{1,0:T(8,128)}, f32[1024,16]{1,0:T(8,128)}) fusion(f32[1024,16]{1,0:T(8,128)S(1)} %copy.40), kind=kLoop, calls=%fused_computation.14 | loop fusion | flops 32768 | bytes 196608 | tf_op jit(solution)/shard_map/neg | solution.py:293
  76.7 9.3 %chirp.2.tab = bf16[8,2,128,2048]{3,2,1,0:T(8,128)(2,1)} custom-call(f32[1024,16]{1,0:T(8,128)} %get-tuple-element.26.a_re, f32[1024,16]{1,0:T(8,128)} %get-tuple-element.25.a_im, f32[1024,128]{1,0:T(8,128)} %get-tuple-element.30.b_re, f32[1024,128]{1,0:T(8,128)} %get-tuple-element.29.b_im), custom_call_target="tpu_custom_call" | custom-call | flops 16777216 | bytes 8388608 | tf_op jit(solution)/shard_map/chirp/pallas_call | solution.py:305
  87.6 6.1 %rows.2 = bf16[8,2,2,128,128]{4,3,2,1,0:T(8,128)(2,1)} custom-call(f32[2,4]{1,0:T(2,128)} %pad_maximum_fusion.5.mix, bf16[8,2,128,2048]{3,2,1,0:T(8,128)(2,1)} %chirp.2.tab, bf16[8,256,256]{2,1,0:T(8,128)(2,1)} %copy-done.1), custom_call_target="tpu_custom_call" | custom-call | tf_op jit(solution)/shard_map/rows/pallas_call | solution.py:384
  93.6 4.2 %all-to-all-start.1 = ((bf16[8,2,2,128,128]{4,3,2,1,0:T(8,128)(2,1)}), bf16[8,2,2,128,128]{4,3,2,1,0:T(8,128)(2,1)S(1)}, u32[]{:S(2)}, u32[]{:S(2)}) async-start(bf16[8,2,2,128,128]{4,3,2,1,0:T(8,128)(2,1)} %rows.2), calls=%async_computation.1 | async-start | bytes 2097152 | tf_op jit(solution)/shard_map/all_to_all | solution.py:397
  98.1 1.9 sine_negate_fusion.2
  101.7 3.8 %chirp.3.tab = bf16[1,2,512,1024]{3,2,1,0:T(8,128)(2,1)} custom-call(f32[512,8]{1,0:T(8,128)} %get-tuple-element.28.a_re, f32[512,8]{1,0:T(8,128)} %get-tuple-element.27.a_im, f32[512,128]{1,0:T(8,128)} %get-tuple-element.32.b_re, f32[512,128]{1,0:T(8,128)} %get-tuple-element.31.b_im), custom_call_target="tpu_custom_call" | custom-call | flops 4194304 | bytes 2097152 | tf_op jit(solution)/shard_map/chirp/pallas_call | solution.py:305
  105.5 7.7 %all-to-all-done.1.g = bf16[8,2,2,128,128]{4,3,2,1,0:T(8,128)(2,1)S(1)} async-done(((bf16[8,2,2,128,128]{4,3,2,1,0:T(8,128)(2,1)}), bf16[8,2,2,128,128]{4,3,2,1,0:T(8,128)(2,1)S(1)}, u32[]{:S(2)}, u32[]{:S(2)}) %all-to-all-start.1) | async-done | bytes 1048608 | tf_op jit(solution)/shard_map/all_to_all | solution.py:397
  114.2 6.0 %cols.2 = bf16[4,4,2,128,256]{4,3,2,1,0:T(8,128)(2,1)} custom-call(bf16[8,2,2,128,128]{4,3,2,1,0:T(8,128)(2,1)} %copy-done.3, bf16[1,2,512,1024]{3,2,1,0:T(8,128)(2,1)} %chirp.3.tab), custom_call_target="tpu_custom_call" | custom-call | flops 4294967296 | bytes 2097152 | tf_op jit(solution)/shard_map/cols/pallas_call | solution.py:398
  121.5 18.4 %all_to_all.20.v = bf16[8,256,256]{2,1,0:T(8,128)(2,1)} all-to-all(bf16[8,256,256]{2,1,0:T(8,128)(2,1)S(1)} %copy-done.2), channel_id=1, replica_groups=mesh['gx'=8,'gy'=4] {'gx'}, dimensions={0} | all-to-all | bytes 2097152 | tf_op jit(solution)/shard_map/all_to_all | solution.py:383
  139.9 6.1 %rows.3 = bf16[8,2,2,128,128]{4,3,2,1,0:T(8,128)(2,1)} custom-call(f32[2,4]{1,0:T(2,128)} %pad_maximum_fusion.5.mix, bf16[8,2,128,2048]{3,2,1,0:T(8,128)(2,1)} %chirp.2.tab, bf16[8,256,256]{2,1,0:T(8,128)(2,1)} %all_to_all.20.v), custom_call_target="tpu_custom_call" | custom-call | tf_op jit(solution)/shard_map/rows/pallas_call | solution.py:384
  146.0 19.6 %all_to_all.21.g = bf16[8,2,2,128,128]{4,3,2,1,0:T(8,128)(2,1)} all-to-all(bf16[8,2,2,128,128]{4,3,2,1,0:T(8,128)(2,1)} %rows.3), channel_id=1, replica_groups=mesh['gx'=8,'gy'=4] {'gx'}, dimensions={0} | all-to-all | bytes 2097152 | tf_op jit(solution)/shard_map/all_to_all | solution.py:397
  165.5 6.0 %cols.3 = bf16[4,4,2,128,256]{4,3,2,1,0:T(8,128)(2,1)} custom-call(bf16[8,2,2,128,128]{4,3,2,1,0:T(8,128)(2,1)} %all_to_all.21.g, bf16[1,2,512,1024]{3,2,1,0:T(8,128)(2,1)} %chirp.3.tab), custom_call_target="tpu_custom_call" | custom-call | flops 4294967296 | bytes 2097152 | tf_op jit(solution)/shard_map/cols/pallas_call | solution.py:398
  172.8 40.9 %reduce-scatter.5.cloned.1.call-done = bf16[1,4,2,128,256]{4,3,2,1,0:T(8,128)(2,1)} async-done(((bf16[4,4,2,128,256]{4,3,2,1,0:T(8,128)(2,1)}), bf16[1,4,2,128,256]{4,3,2,1,0:T(8,128)(2,1)}) %reduce-scatter.5.cloned.1.call-update) | async-done | bytes 524304 | tf_op jit(solution)/shard_map/reduce_scatter | solution.py:414
  215.0 2.9 %copy.42 = f32[128,2,4,2,256]{4,3,2,1,0:T(2,128)} copy(f32[128,2,4,2,256]{4,0,3,2,1:T(8,128)S(1)} %pad_maximum_fusion.1) | data formatting | bytes 4194304 | tf_op jit(solution)/shard_map/concatenate | solution.py:417
  (61 shorter events, 20.9 us)
Async XLA Ops:
  13.2 12.1 %copy-start.4 = (f32[2]{0:T(128)S(1)}, f32[2]{0:T(128)}, u32[]{:S(2)}) copy-start(f32[2]{0:T(128)} %param.13) | copy-start | bytes 28
  15.4 10.5 %collective-permute-start = (f32[21,2,256]{2,1,0:T(2,128)S(1)}, f32[21,2,256]{2,1,0:T(2,128)S(1)}, u32[]{:S(2)}, u32[]{:S(2)}) collective-permute-start(f32[21,2,256]{2,1,0:T(2,128)S(1)} %maximum_bitcast_fusion), channel_id=1, source_target_pairs={{1,0},{2,1},{3,2},{5,4},{6,5},{7,6},{9,8},{10,9},{11,10},{13,12},{... | collective-permute-start | bytes 129032 | tf_op jit(solution)/shard_map/ppermute | solution.py:36
  17.6 10.6 %collective-permute-start.1 = (f32[21,2,256]{2,1,0:T(2,128)S(1)}, f32[21,2,256]{2,1,0:T(2,128)S(1)}, u32[]{:S(2)}, u32[]{:S(2)}) collective-permute-start(f32[21,2,256]{2,1,0:T(2,128)S(1)} %maximum_bitcast_fusion.1), channel_id=1, source_target_pairs={{0,1},{1,2},{2,3},{4,5},{5,6},{6,7},{8,9},{9,10},{10,11},{12,13},{... | collective-permute-start | bytes 129032 | tf_op jit(solution)/shard_map/ppermute | solution.py:36
  34.0 6.5 %copy-start = (f32[21,256,128]{2,1,0:T(8,128)}, f32[21,256,128]{2,1,0:T(8,128)S(1)}, u32[]{:S(2)}) copy-start(f32[21,256,128]{2,1,0:T(8,128)S(1)} %pad_maximum_fusion.colh) | copy-start | bytes 8257540
  34.1 4.4 %collective-permute-start.2 = (f32[21,2,640]{2,1,0:T(2,128)S(1)}, f32[21,2,640]{2,1,0:T(2,128)S(1)}, u32[]{:S(2)}, u32[]{:S(2)}) collective-permute-start(f32[21,2,640]{2,1,0:T(2,128)S(1)} %pad_maximum_fusion.3), channel_id=1, source_target_pairs={{4,0},{8,4},{12,8},{16,12},{20,16},{24,20},{28,24},{5,1},{9,5},{13... | collective-permute-start | bytes 322568 | tf_op jit(solution)/shard_map/ppermute | solution.py:36
  35.5 4.0 %collective-permute-start.3 = (f32[21,2,640]{2,1,0:T(2,128)S(1)}, f32[21,2,640]{2,1,0:T(2,128)S(1)}, u32[]{:S(2)}, u32[]{:S(2)}) collective-permute-start(f32[21,2,640]{2,1,0:T(2,128)S(1)} %pad_maximum_fusion.4), channel_id=1, source_target_pairs={{0,4},{4,8},{8,12},{12,16},{16,20},{20,24},{24,28},{1,5},{5,9},{9,... | collective-permute-start | bytes 322568 | tf_op jit(solution)/shard_map/ppermute | solution.py:36
  63.2 23.4 %all-to-all-start = ((bf16[8,256,256]{2,1,0:T(8,128)(2,1)}), bf16[8,256,256]{2,1,0:T(8,128)(2,1)S(1)}, u32[]{:S(2)}, u32[]{:S(2)}) async-start(bf16[8,256,256]{2,1,0:T(8,128)(2,1)} %get-tuple-element.9), calls=%async_computation | async-start | bytes 2097152 | tf_op jit(solution)/shard_map/all_to_all | solution.py:383
  86.6 1.0 copy-start.1
  93.6 19.6 %all-to-all-start.1 = ((bf16[8,2,2,128,128]{4,3,2,1,0:T(8,128)(2,1)}), bf16[8,2,2,128,128]{4,3,2,1,0:T(8,128)(2,1)S(1)}, u32[]{:S(2)}, u32[]{:S(2)}) async-start(bf16[8,2,2,128,128]{4,3,2,1,0:T(8,128)(2,1)} %rows.2), calls=%async_computation.1 | async-start | bytes 2097152 | tf_op jit(solution)/shard_map/all_to_all | solution.py:397
  97.8 73.8 %reduce-scatter.3.cloned.1.call-start = ((), (), s32[]{:S(2)}) async-start(), calls=%async_computation.6 | async-start | bytes 2621440 | tf_op jit(solution)/shard_map/reduce_scatter | solution.py:414
  113.2 1.0 copy-start.3
  120.2 1.2 copy-start.2
  120.3 93.4 %reduce-scatter.5.cloned.1.call-start = ((), (), s32[]{:S(2)}) async-start(), calls=%async_computation.7 | async-start | bytes 2621440 | tf_op jit(solution)/shard_map/reduce_scatter | solution.py:414
Sparse Core Ops, SparseCore 0:
  120.4 41.9 reduce-scatter.2
  171.7 41.9 reduce-scatter.4
